TPU v7x, 32 devices: a whole 2x2x4 slice. The times are simulated.
32 devices in a mesh: gx: 4 (over z), gy: 4 (over y, x), gz: 2 (over core).
Axes of the slice: x: 2, y: 2, z: 4, core: 2. Of those that a mesh axis runs over, the one named last changes fastest.
Arguments:
- source_points: float32 [3, 13, 4, 16, 4, 512], P(None, None, 'gx', 'gy', 'gz'), may hold values from -3 to 3
- target_points: float32 [3, 13, 4, 16, 4, 512], P(None, None, 'gx', 'gy', 'gz'), may hold values from -3 to 3
- normals: float32 [3, 13, 4, 16, 4, 512], P(None, None, 'gx', 'gy', 'gz'), may hold values from -4 to 4
- weights: float32 [13, 4, 16, 4, 512], P(None, 'gx', 'gy', 'gz'), may hold values from 0.1 to 1
- blocks: int32 [13, 4, 16, 4], P(None, 'gx', 'gy', 'gz'), may hold values from 0 to 2
- affines: float32 [12, 4, 16, 4], P(None, 'gx', 'gy', 'gz'), may hold values from -0.5 to 0.5
- anchor: int32 [1], replicated, may hold values from 0 to 255
Outputs:
- update: float32 [12, 4, 16, 4], P(None, 'gx', 'gy', 'gz')
- residual: float32 [12, 4, 16, 4], P(None, 'gx', 'gy', 'gz')
Inputs may be any that keep to these rules, and one draw needn't show every extreme that they name: `blocks`: number of 256-point correspondence blocks of the correlation; entries of correlations whose second tile lies outside the grid are not read. `anchor`: a tile index (x 16 + y) * 4 + z.
All inputs are finite; a program needn't handle non-finite values.
Results may differ from a plain program's by a relative error of at most 0.0003.
Values sent between devices are 32-bit elements; how exact they have to be, the bound alone decides.
A program may use at most 128 MiB of HBM per device.

v0:
```python
import jax
import jax.numpy as jnp
from jax import lax
from jax.sharding import PartitionSpec as P

BLOCK = 256
ITERS = 10
SPACING = 0.5
DAMPING = 1.0
OFFSETS = (
    (1, 0, 0),
    (0, 1, 0),
    (0, 0, 1),
    (1, 1, -1),
    (1, -1, 1),
    (-1, 1, 1),
    (1, 1, 0),
    (1, 0, 1),
    (0, 1, 1),
    (1, 1, 1),
    (1, -1, 0),
    (0, 1, -1),
    (-1, 0, 1),
)


def padded(value, sides, width):
    for axis, dim in sides:
        devices, length = (lax.axis_size(axis), value.shape[dim])
        up = [(i, (i + 1) % devices) for i in range(devices - 1)]
        down = [(j, i) for i, j in up]
        last = lax.slice_in_dim(value, length - width, length, axis=dim)
        first = lax.slice_in_dim(value, 0, width, axis=dim)
        before = lax.ppermute(last, axis, up)
        after = lax.ppermute(first, axis, down)
        value = jnp.concatenate([before, value, after], axis=dim)
    return value


def spot(offset, rank, first, lengths):
    picks = [slice(None)] * rank
    for axis in range(3):
        picks[first + axis] = slice(1 + offset[axis], 1 + offset[axis] + lengths[axis])
    return tuple(picks)


def window(values, offset, first):
    lengths = tuple((values.shape[first + axis] - 2 for axis in range(3)))
    return values[spot(offset, values.ndim, first, lengths)]


def lifted(points):
    return jnp.concatenate([points, jnp.ones((1,) + points.shape[1:], points.dtype)], axis=0)


def mapped(affine, lifted_points):
    matrix = affine.reshape((3, 4) + affine.shape[1:]) + jnp.eye(3, 4, dtype=affine.dtype).reshape(
        3, 4, 1, 1, 1
    )
    return jnp.einsum("cexyz,exyzp->cxyzp", matrix, lifted_points, precision=lax.Precision.HIGHEST)


def correlation_terms(source, target, normal, weight, affine_here, affine_there, offset):
    exact = lax.Precision.HIGHEST
    source_lift = lifted(source)
    target_lift = lifted(target)
    stride = jnp.asarray(offset, source.dtype).reshape(3, 1, 1, 1, 1) * SPACING
    misfit = jnp.sum(
        normal * (mapped(affine_here, source_lift) - mapped(affine_there, target_lift) - stride),
        axis=0,
    )
    layout = (12,) + source.shape[1:]
    rows_here = (normal[:, None] * source_lift[None]).reshape(layout)
    rows_there = -(normal[:, None] * target_lift[None]).reshape(layout)
    weighted_here = rows_here * weight
    weighted_there = rows_there * weight
    block_here = jnp.einsum("axyzp,bxyzp->abxyz", weighted_here, rows_here, precision=exact)
    block_pair = jnp.einsum("axyzp,bxyzp->abxyz", weighted_here, rows_there, precision=exact)
    block_there = jnp.einsum("axyzp,bxyzp->abxyz", weighted_there, rows_there, precision=exact)
    pull_here = jnp.einsum("axyzp,xyzp->axyz", weighted_here, misfit, precision=exact)
    pull_there = jnp.einsum("axyzp,xyzp->axyz", weighted_there, misfit, precision=exact)
    return (block_here, block_pair, block_there, pull_here, pull_there)


def invert_blocks(blocks):
    left = blocks
    right = jnp.broadcast_to(
        jnp.eye(12, dtype=blocks.dtype).reshape((12, 12) + (1,) * (blocks.ndim - 2)), blocks.shape
    )
    for pivot in range(12):
        factor = 1.0 / left[pivot, pivot]
        row_left = left[pivot] * factor
        row_right = right[pivot] * factor
        column = left[:, pivot]
        left = left - column[:, None] * row_left[None]
        right = right - column[:, None] * row_right[None]
        left = left.at[pivot].set(row_left)
        right = right.at[pivot].set(row_right)
    return right


def fold_back(extended):
    rims = jnp.concatenate([extended[:, :1], extended[:, -1:]], axis=1)
    came = padded(rims, (("gx", 1),), 1)
    inner = extended[:, 1:-1]
    inner = inner.at[:, :1].add(came[:, :1]).at[:, -1:].add(came[:, -1:])
    rims = jnp.concatenate([inner[:, :, :1], inner[:, :, -1:]], axis=2)
    came = padded(rims, (("gy", 2),), 1)
    inner = inner[:, :, 1:-1]
    inner = inner.at[:, :, :1].add(came[:, :, :1]).at[:, :, -1:].add(came[:, :, -1:])
    rims = jnp.concatenate([inner[:, :, :, :1], inner[:, :, :, -1:]], axis=3)
    came = padded(rims, (("gz", 3),), 1)
    inner = inner[:, :, :, 1:-1]
    return inner.at[:, :, :, :1].add(came[:, :, :, :1]).at[:, :, :, -1:].add(came[:, :, :, -1:])


def beside_all(vector):
    return padded(vector, (("gx", 1), ("gy", 2), ("gz", 3)), 1)


def both_products(residual, scaled, image):
    return lax.psum((jnp.sum(residual * scaled), jnp.sum(image * scaled)), ("gx", "gy", "gz"))


def on_device(source_points, target_points, normals, weights, blocks, affines, anchor):
    exact = lax.Precision.HIGHEST
    directions = source_points.shape[1]
    tile_x, tile_y, tile_z = (
        source_points.shape[2],
        source_points.shape[3],
        source_points.shape[4],
    )
    points = source_points.shape[5]
    lengths = (tile_x, tile_y, tile_z)
    span_x = tile_x * lax.axis_size("gx")
    span_y = tile_y * lax.axis_size("gy")
    span_z = tile_z * lax.axis_size("gz")
    wide_x = lax.axis_index("gx") * tile_x - 1 + jnp.arange(tile_x + 2, dtype=jnp.int32)
    wide_y = lax.axis_index("gy") * tile_y - 1 + jnp.arange(tile_y + 2, dtype=jnp.int32)
    wide_z = lax.axis_index("gz") * tile_z - 1 + jnp.arange(tile_z + 2, dtype=jnp.int32)
    inside_x = ((wide_x >= 0) & (wide_x < span_x)).astype(jnp.float32).reshape(-1, 1, 1)
    inside_y = ((wide_y >= 0) & (wide_y < span_y)).astype(jnp.float32).reshape(1, -1, 1)
    inside_z = ((wide_z >= 0) & (wide_z < span_z)).astype(jnp.float32).reshape(1, 1, -1)
    inside_wide = inside_x * inside_y * inside_z
    flat_wide = (
        wide_x.reshape(-1, 1, 1) * span_y + wide_y.reshape(1, -1, 1)
    ) * span_z + wide_z.reshape(1, 1, -1)
    keep_wide = inside_wide * (flat_wide != anchor[0]).astype(jnp.float32)
    keep = keep_wide[1:-1, 1:-1, 1:-1]
    gathered = (
        padded(
            target_points.reshape((3 * directions, tile_x, tile_y, tile_z, points)),
            (("gx", 1), ("gy", 2), ("gz", 3)),
            1,
        ),
        padded(
            affines.reshape((12, tile_x, tile_y, tile_z, 1)), (("gx", 1), ("gy", 2), ("gz", 3)), 1
        ),
    )
    target_wide = gathered[0].reshape((3, directions) + gathered[0].shape[1:])
    affine_wide = gathered[1][..., 0]
    slots = jnp.arange(points, dtype=jnp.int32).reshape(1, 1, 1, points)
    extended = (tile_x + 2, tile_y + 2, tile_z + 2)
    diag = jnp.zeros((12, 12) + lengths, jnp.float32)
    pull = jnp.zeros((12,) + lengths, jnp.float32)
    back_blocks = jnp.zeros((156,) + extended, jnp.float32)
    pairs = []
    for index, offset in enumerate(OFFSETS):
        inside = window(inside_wide, offset, 0)
        live = (slots < BLOCK * blocks[index][..., None]).astype(jnp.float32) * inside[..., None]
        target = window(target_wide[:, index], offset, 1)
        block_here, block_pair, block_there, pull_here, pull_there = correlation_terms(
            source_points[:, index],
            target,
            normals[:, index],
            weights[index] * live,
            affines,
            window(affine_wide, offset, 1),
            offset,
        )
        block_pair = block_pair * (keep * window(keep_wide, offset, 0))
        diag = diag + block_here
        pull = pull + pull_here
        pairs.append(block_pair)
        place = spot(offset, 4, 1, lengths)
        back_blocks = back_blocks.at[place].add(
            jnp.concatenate([block_there.reshape((144,) + lengths), pull_there], axis=0)
        )
    coupling = jnp.stack(pairs)
    folded = fold_back(back_blocks)
    diag = diag + folded[:144].reshape((12, 12) + lengths)
    pull = pull + folded[144:156]
    identity = jnp.eye(12, dtype=jnp.float32).reshape(12, 12, 1, 1, 1)
    diag = keep * (diag + DAMPING * identity) + (1.0 - keep) * identity
    rhs = -(keep * pull)
    inverse = invert_blocks(diag)

    def operate(vector):
        wide = beside_all(vector)
        ahead = jnp.stack([window(wide, offset, 1) for offset in OFFSETS])
        result = jnp.einsum("abxyz,bxyz->axyz", diag, vector, precision=exact)
        result = result + jnp.einsum("dabxyz,dbxyz->axyz", coupling, ahead, precision=exact)
        sent = jnp.einsum("dbaxyz,bxyz->daxyz", coupling, vector, precision=exact)
        back = jnp.zeros((12,) + extended, jnp.float32)
        for index, offset in enumerate(OFFSETS):
            back = back.at[spot(offset, 4, 1, lengths)].add(sent[index])
        return result + fold_back(back)

    def precondition(vector):
        return jnp.einsum("abxyz,bxyz->axyz", inverse, vector, precision=exact)

    update = jnp.zeros_like(rhs)
    residual = rhs
    scaled = precondition(residual)
    image = operate(scaled)
    inner, product = both_products(residual, scaled, image)
    alpha = inner / product
    direction, along = (scaled, image)
    for step in range(ITERS):
        update = update + alpha * direction
        residual = residual - alpha * along
        if step + 1 < ITERS:
            scaled = precondition(residual)
            image = operate(scaled)
            inner_next, product = both_products(residual, scaled, image)
            ratio = inner_next / inner
            alpha = inner_next / (product - ratio * inner_next / alpha)
            direction = scaled + ratio * direction
            along = image + ratio * along
            inner = inner_next
    return (update, residual)


def solution(mesh):
    placed = (
        P(None, None, "gx", "gy", "gz", None),
        P(None, None, "gx", "gy", "gz", None),
        P(None, None, "gx", "gy", "gz", None),
        P(None, "gx", "gy", "gz", None),
        P(None, "gx", "gy", "gz"),
        P(None, "gx", "gy", "gz"),
        P(),
    )
    return jax.shard_map(
        on_device,
        mesh=mesh,
        in_specs=placed,
        out_specs=(P(None, "gx", "gy", "gz"), P(None, "gx", "gy", "gz")),
        check_vma=False,
    )
```

profile of v0, /device:TPU:0, one launch (start us, length us, event | category | flops | bytes accessed | tf_op | source)
XLA Modules:
  0.0 1302.6 jit_solution(10599703377848781927)
XLA Ops:
  0.6 5.1 collective-permute-start
  7.8 5.1 collective-permute-start.6
  132.2 4.6 collective-permute-start.8
  162.1 5.6 pad_maximum_fusion
  199.2 11.4 fusion.203
  355.0 5.1 collective-permute-start.19
  360.4 5.7 fusion.452
  377.3 4.5 collective-permute-start.21
  393.3 5.3 collective-permute-done.27
  404.8 41.6 %all-reduce.46 = (f32[]{:T(128)}, f32[]{:T(128)}) all-reduce(f32[]{:T(128)} %get-tuple-element.2981, f32[]{:T(128)} %get-tuple-element.2980), channel_id=1, replica_groups=mesh['gx'=4,'gy'=4,'gz'=2] {'gx','gy','gz'}, use_global_device_ids=true, to_apply=%region_14.0 | all-reduce | flops 2 | bytes 16 | tf_op jit(solution)/shard_map/psum | solution.py:122
  449.3 4.5 collective-permute-start.31
  454.0 5.7 fusion.446
  468.7 4.8 collective-permute-start.33
  479.3 4.8 collective-permute-start.38
  485.4 5.3 collective-permute-done.39
  497.0 41.6 %all-reduce.45 = (f32[]{:T(128)}, f32[]{:T(128)}) all-reduce(f32[]{:T(128)} %get-tuple-element.2979, f32[]{:T(128)} %get-tuple-element.2978), channel_id=1, replica_groups=mesh['gx'=4,'gy'=4,'gz'=2] {'gx','gy','gz'}, use_global_device_ids=true, to_apply=%region_18.0 | all-reduce | flops 2 | bytes 16 | tf_op jit(solution)/shard_map/psum | solution.py:122
  544.7 4.5 collective-permute-start.43
  549.5 5.7 fusion.440
  564.1 4.8 collective-permute-start.45
  574.7 4.8 collective-permute-start.50
  580.9 5.3 collective-permute-done.51
  592.4 41.6 %all-reduce.44 = (f32[]{:T(128)}, f32[]{:T(128)}) all-reduce(f32[]{:T(128)} %get-tuple-element.2977, f32[]{:T(128)} %get-tuple-element.2976), channel_id=1, replica_groups=mesh['gx'=4,'gy'=4,'gz'=2] {'gx','gy','gz'}, use_global_device_ids=true, to_apply=%region_22.0 | all-reduce | flops 2 | bytes 16 | tf_op jit(solution)/shard_map/psum | solution.py:122
  639.4 4.5 collective-permute-start.55
  644.2 5.7 fusion.434
  658.9 4.8 collective-permute-start.57
  669.4 4.8 collective-permute-start.62
  675.6 5.3 collective-permute-done.63
  687.6 41.6 %all-reduce.43 = (f32[]{:T(128)}, f32[]{:T(128)}) all-reduce(f32[]{:T(128)} %get-tuple-element.2975, f32[]{:T(128)} %get-tuple-element.2974), channel_id=1, replica_groups=mesh['gx'=4,'gy'=4,'gz'=2] {'gx','gy','gz'}, use_global_device_ids=true, to_apply=%region_26.0 | all-reduce | flops 2 | bytes 16 | tf_op jit(solution)/shard_map/psum | solution.py:122
  734.5 4.5 collective-permute-start.67
  739.2 5.7 fusion.428
  753.9 4.8 collective-permute-start.69
  764.5 4.8 collective-permute-start.74
  770.6 5.3 collective-permute-done.75
  782.1 41.6 %all-reduce.42 = (f32[]{:T(128)}, f32[]{:T(128)}) all-reduce(f32[]{:T(128)} %get-tuple-element.2973, f32[]{:T(128)} %get-tuple-element.2972), channel_id=1, replica_groups=mesh['gx'=4,'gy'=4,'gz'=2] {'gx','gy','gz'}, use_global_device_ids=true, to_apply=%region_30.0 | all-reduce | flops 2 | bytes 16 | tf_op jit(solution)/shard_map/psum | solution.py:122
  829.1 4.5 collective-permute-start.79
  833.8 5.7 fusion.422
  848.5 4.8 collective-permute-start.81
  859.1 4.8 collective-permute-start.86
  865.2 5.3 collective-permute-done.87
  877.0 41.6 %all-reduce.41 = (f32[]{:T(128)}, f32[]{:T(128)}) all-reduce(f32[]{:T(128)} %get-tuple-element.2971, f32[]{:T(128)} %get-tuple-element.2970), channel_id=1, replica_groups=mesh['gx'=4,'gy'=4,'gz'=2] {'gx','gy','gz'}, use_global_device_ids=true, to_apply=%region_34.0 | all-reduce | flops 2 | bytes 16 | tf_op jit(solution)/shard_map/psum | solution.py:122
  923.9 4.5 collective-permute-start.91
  928.6 5.7 fusion.416
  943.3 4.8 collective-permute-start.93
  953.9 4.8 collective-permute-start.98
  960.0 5.3 collective-permute-done.99
  971.5 41.6 %all-reduce.40 = (f32[]{:T(128)}, f32[]{:T(128)}) all-reduce(f32[]{:T(128)} %get-tuple-element.2969, f32[]{:T(128)} %get-tuple-element.2968), channel_id=1, replica_groups=mesh['gx'=4,'gy'=4,'gz'=2] {'gx','gy','gz'}, use_global_device_ids=true, to_apply=%region_38.0 | all-reduce | flops 2 | bytes 16 | tf_op jit(solution)/shard_map/psum | solution.py:122
  1018.5 4.5 collective-permute-start.103
  1023.2 5.7 fusion.410
  1037.9 4.8 collective-permute-start.105
  1048.5 4.8 collective-permute-start.110
  1054.6 5.3 collective-permute-done.111
  1066.4 41.6 %all-reduce.39 = (f32[]{:T(128)}, f32[]{:T(128)}) all-reduce(f32[]{:T(128)} %get-tuple-element.2967, f32[]{:T(128)} %get-tuple-element.2966), channel_id=1, replica_groups=mesh['gx'=4,'gy'=4,'gz'=2] {'gx','gy','gz'}, use_global_device_ids=true, to_apply=%region_42.0 | all-reduce | flops 2 | bytes 16 | tf_op jit(solution)/shard_map/psum | solution.py:122
  1113.3 4.5 collective-permute-start.115
  1118.1 5.7 fusion.404
  1132.7 4.8 collective-permute-start.117
  1143.3 4.8 collective-permute-start.122
  1149.5 5.3 collective-permute-done.123
  1161.0 41.6 %all-reduce.38 = (f32[]{:T(128)}, f32[]{:T(128)}) all-reduce(f32[]{:T(128)} %get-tuple-element.2965, f32[]{:T(128)} %get-tuple-element.2964), channel_id=1, replica_groups=mesh['gx'=4,'gy'=4,'gz'=2] {'gx','gy','gz'}, use_global_device_ids=true, to_apply=%region_46.0 | all-reduce | flops 2 | bytes 16 | tf_op jit(solution)/shard_map/psum | solution.py:122
  1207.9 4.5 collective-permute-start.127
  1212.7 5.7 fusion.398
  1227.4 4.8 collective-permute-start.129
  1237.9 4.8 collective-permute-start.134
  1244.1 5.3 collective-permute-done.135
  1255.7 41.6 %all-reduce.37 = (f32[]{:T(128)}, f32[]{:T(128)}) all-reduce(f32[]{:T(128)} %get-tuple-element.2963, f32[]{:T(128)} %get-tuple-element.2962), channel_id=1, replica_groups=mesh['gx'=4,'gy'=4,'gz'=2] {'gx','gy','gz'}, use_global_device_ids=true, to_apply=%region_50.0 | all-reduce | flops 2 | bytes 16 | tf_op jit(solution)/shard_map/psum | solution.py:122
  (1674 shorter events, 561.1 us)
Async XLA Ops:
  0.6 51.8 %collective-permute-start = (f32[39,1,4,2,512]{4,3,2,1,0:T(2,128)}, f32[39,1,4,2,512]{4,3,2,1,0:T(2,128)S(1)}, u32[]{:S(2)}, u32[]{:S(2)}) collective-permute-start(f32[39,1,4,2,512]{4,3,2,1,0:T(2,128)} %bitcast.2152), channel_id=1, source_target_pairs={{0,8},{8,16},{16,24},{1,9},{9,17},{17,25},{2,10},{10,18},{18,26},{... | collective-permute-start | bytes 1916936 | tf_op jit(solution)/shard_map/ppermute | solution.py:34
  5.8 46.6 %collective-permute-start.1 = (f32[39,1,4,2,512]{4,3,2,1,0:T(2,128)}, f32[39,1,4,2,512]{4,3,2,1,0:T(2,128)S(1)}, u32[]{:S(2)}, u32[]{:S(2)}) collective-permute-start(f32[39,1,4,2,512]{4,3,2,1,0:T(2,128)} %bitcast.2153), channel_id=1, source_target_pairs={{8,0},{16,8},{24,16},{9,1},{17,9},{25,17},{10,2},{18,10},{26,18},{... | collective-permute-start | bytes 1916936 | tf_op jit(solution)/shard_map/ppermute | solution.py:35
  7.8 123.7 %collective-permute-start.6 = (f32[12,1,4,2,1]{0,2,4,3,1:T(4,128)S(1)}, f32[12,1,4,2,1]{0,2,4,3,1:T(4,128)}, u32[]{:S(2)}, u32[]{:S(2)}) collective-permute-start(f32[12,1,4,2,1]{0,2,4,3,1:T(4,128)S(1)} %bitcast.2434), channel_id=1, source_target_pairs={{0,8},{8,16},{16,24},{1,9},{9,17},{17,25},{2,10},{10,18},{18,26},{... | collective-permute-start | bytes 1160 | tf_op jit(solution)/shard_map/ppermute | solution.py:34
  12.9 118.5 %collective-permute-start.7 = (f32[12,1,4,2,1]{0,2,4,3,1:T(4,128)S(1)}, f32[12,1,4,2,1]{0,2,4,3,1:T(4,128)}, u32[]{:S(2)}, u32[]{:S(2)}) collective-permute-start(f32[12,1,4,2,1]{0,2,4,3,1:T(4,128)S(1)} %bitcast.2435), channel_id=1, source_target_pairs={{8,0},{16,8},{24,16},{9,1},{17,9},{25,17},{10,2},{18,10},{26,18},{... | collective-permute-start | bytes 1160 | tf_op jit(solution)/shard_map/ppermute | solution.py:35
  53.8 64.2 %collective-permute-start.2 = (f32[39,3,1,2,512]{4,3,2,1,0:T(2,128)}, f32[39,3,1,2,512]{4,3,2,1,0:T(2,128)S(1)}, u32[]{:S(2)}, u32[]{:S(2)}) collective-permute-start(f32[39,3,1,2,512]{4,3,2,1,0:T(2,128)} %get-tuple-element.3030), channel_id=1, source_target_pairs={{0,2},{2,4},{4,6},{1,3},{3,5},{5,7},{8,10},{10,12},{12,14},{9,11},... | collective-permute-start | bytes 1437704 | tf_op jit(solution)/shard_map/ppermute | solution.py:34
  57.2 60.7 %collective-permute-start.3 = (f32[39,3,1,2,512]{4,3,2,1,0:T(2,128)}, f32[39,3,1,2,512]{4,3,2,1,0:T(2,128)S(1)}, u32[]{:S(2)}, u32[]{:S(2)}) collective-permute-start(f32[39,3,1,2,512]{4,3,2,1,0:T(2,128)} %get-tuple-element.3031), channel_id=1, source_target_pairs={{2,0},{4,2},{6,4},{3,1},{5,3},{7,5},{10,8},{12,10},{14,12},{11,9},... | collective-permute-start | bytes 1437704 | tf_op jit(solution)/shard_map/ppermute | solution.py:35
  123.4 38.7 %collective-permute-start.4 = (f32[39,3,6,1,512]{4,3,2,1,0:T(1,128)}, f32[39,3,6,1,512]{4,3,2,1,0:T(1,128)}, u32[]{:S(2)}, u32[]{:S(2)}) collective-permute-start(f32[39,3,6,1,512]{4,3,2,1,0:T(1,128)} %get-tuple-element.3028), channel_id=1, source_target_pairs={{0,1},{2,3},{4,5},{6,7},{8,9},{10,11},{12,13},{14,15},{16,17},{18,... | collective-permute-start | bytes 4313096 | tf_op jit(solution)/shard_map/ppermute | solution.py:34
  125.8 36.3 %collective-permute-start.5 = (f32[39,3,6,1,512]{4,3,2,1,0:T(1,128)}, f32[39,3,6,1,512]{4,3,2,1,0:T(1,128)}, u32[]{:S(2)}, u32[]{:S(2)}) collective-permute-start(f32[39,3,6,1,512]{4,3,2,1,0:T(1,128)} %get-tuple-element.3029), channel_id=1, source_target_pairs={{1,0},{3,2},{5,4},{7,6},{9,8},{11,10},{13,12},{15,14},{17,16},{19,... | collective-permute-start | bytes 4313096 | tf_op jit(solution)/shard_map/ppermute | solution.py:35
  276.6 50.9 %collective-permute-start.12 = (f32[156,1,6,4]{0,3,2,1:T(4,128)S(1)}, f32[156,1,6,4]{0,3,2,1:T(4,128)S(1)}, u32[]{:S(2)}, u32[]{:S(2)}) collective-permute-start(f32[156,1,6,4]{0,3,2,1:T(4,128)S(1)} %get-tuple-element.3070), channel_id=1, source_target_pairs={{0,8},{8,16},{16,24},{1,9},{9,17},{17,25},{2,10},{10,18},{18,26},{... | collective-permute-start | bytes 44936 | tf_op jit(solution)/shard_map/ppermute | solution.py:34
  281.1 46.4 %collective-permute-start.13 = (f32[156,1,6,4]{0,3,2,1:T(4,128)S(1)}, f32[156,1,6,4]{0,3,2,1:T(4,128)S(1)}, u32[]{:S(2)}, u32[]{:S(2)}) collective-permute-start(f32[156,1,6,4]{0,3,2,1:T(4,128)S(1)} %get-tuple-element.3071), channel_id=1, source_target_pairs={{8,0},{16,8},{24,16},{9,1},{17,9},{25,17},{10,2},{18,10},{26,18},{... | collective-permute-start | bytes 44936 | tf_op jit(solution)/shard_map/ppermute | solution.py:35
  353.7 22.3 %collective-permute-start.18 = (f32[12,1,4,2]{0,3,2,1:T(2,128)S(1)}, f32[12,1,4,2]{0,3,2,1:T(2,128)S(1)}, u32[]{:S(2)}, u32[]{:S(2)}) collective-permute-start(f32[12,1,4,2]{0,3,2,1:T(2,128)S(1)} %bitcast.2227), channel_id=1, source_target_pairs={{8,0},{16,8},{24,16},{9,1},{17,9},{25,17},{10,2},{18,10},{26,18},{... | collective-permute-start | bytes 1160 | tf_op jit(solution)/shard_map/ppermute | solution.py:35
  355.0 21.0 %collective-permute-start.19 = (f32[12,1,4,2]{0,3,2,1:T(2,128)S(1)}, f32[12,1,4,2]{0,3,2,1:T(2,128)S(1)}, u32[]{:S(2)}, u32[]{:S(2)}) collective-permute-start(f32[12,1,4,2]{0,3,2,1:T(2,128)S(1)} %bitcast.2228), channel_id=1, source_target_pairs={{0,8},{8,16},{16,24},{1,9},{9,17},{17,25},{2,10},{10,18},{18,26},{... | collective-permute-start | bytes 1160 | tf_op jit(solution)/shard_map/ppermute | solution.py:34
  370.5 17.0 %collective-permute-start.24 = (f32[12,1,6,4]{0,3,2,1:T(4,128)S(1)}, f32[12,1,6,4]{0,3,2,1:T(4,128)S(1)}, u32[]{:S(2)}, u32[]{:S(2)}) collective-permute-start(f32[12,1,6,4]{0,3,2,1:T(4,128)S(1)} %get-tuple-element.3259), channel_id=1, source_target_pairs={{0,8},{8,16},{16,24},{1,9},{9,17},{17,25},{2,10},{10,18},{18,26},{... | collective-permute-start | bytes 3464 | tf_op jit(solution)/shard_map/ppermute | solution.py:34
  383.2 19.8 %collective-permute-start.22 = (f32[12,3,6,1]{0,3,2,1:T(1,128)S(1)}, f32[12,3,6,1]{0,3,2,1:T(1,128)S(1)}, u32[]{:S(2)}, u32[]{:S(2)}) collective-permute-start(f32[12,3,6,1]{0,3,2,1:T(1,128)S(1)} %get-tuple-element.3374), channel_id=1, source_target_pairs={{1,0},{3,2},{5,4},{7,6},{9,8},{11,10},{13,12},{15,14},{17,16},{19,... | collective-permute-start | bytes 2600 | tf_op jit(solution)/shard_map/ppermute | solution.py:35
  384.5 18.5 %collective-permute-start.23 = (f32[12,3,6,1]{0,3,2,1:T(1,128)S(1)}, f32[12,3,6,1]{0,3,2,1:T(1,128)S(1)}, u32[]{:S(2)}, u32[]{:S(2)}) collective-permute-start(f32[12,3,6,1]{0,3,2,1:T(1,128)S(1)} %get-tuple-element.3373), channel_id=1, source_target_pairs={{0,1},{2,3},{4,5},{6,7},{8,9},{10,11},{12,13},{14,15},{16,17},{18,... | collective-permute-start | bytes 2600 | tf_op jit(solution)/shard_map/ppermute | solution.py:34
  448.0 19.4 %collective-permute-start.30 = (f32[12,1,4,2]{0,3,2,1:T(2,128)S(1)}, f32[12,1,4,2]{0,3,2,1:T(2,128)S(1)}, u32[]{:S(2)}, u32[]{:S(2)}) collective-permute-start(f32[12,1,4,2]{0,3,2,1:T(2,128)S(1)} %bitcast.2238), channel_id=1, source_target_pairs={{8,0},{16,8},{24,16},{9,1},{17,9},{25,17},{10,2},{18,10},{26,18},{... | collective-permute-start | bytes 1160 | tf_op jit(solution)/shard_map/ppermute | solution.py:35
  449.3 18.1 %collective-permute-start.31 = (f32[12,1,4,2]{0,3,2,1:T(2,128)S(1)}, f32[12,1,4,2]{0,3,2,1:T(2,128)S(1)}, u32[]{:S(2)}, u32[]{:S(2)}) collective-permute-start(f32[12,1,4,2]{0,3,2,1:T(2,128)S(1)} %bitcast.2239), channel_id=1, source_target_pairs={{0,8},{8,16},{16,24},{1,9},{9,17},{17,25},{2,10},{10,18},{18,26},{... | collective-permute-start | bytes 1160 | tf_op jit(solution)/shard_map/ppermute | solution.py:34
  464.2 15.1 %collective-permute-start.36 = (f32[12,1,6,4]{0,3,2,1:T(4,128)S(1)}, f32[12,1,6,4]{0,3,2,1:T(4,128)S(1)}, u32[]{:S(2)}, u32[]{:S(2)}) collective-permute-start(f32[12,1,6,4]{0,3,2,1:T(4,128)S(1)} %get-tuple-element.3257), channel_id=1, source_target_pairs={{0,8},{8,16},{16,24},{1,9},{9,17},{17,25},{2,10},{10,18},{18,26},{... | collective-permute-start | bytes 3464 | tf_op jit(solution)/shard_map/ppermute | solution.py:34
  474.9 20.3 %collective-permute-start.34 = (f32[12,3,6,1]{0,3,2,1:T(1,128)S(1)}, f32[12,3,6,1]{0,3,2,1:T(1,128)S(1)}, u32[]{:S(2)}, u32[]{:S(2)}) collective-permute-start(f32[12,3,6,1]{0,3,2,1:T(1,128)S(1)} %get-tuple-element.3371), channel_id=1, source_target_pairs={{1,0},{3,2},{5,4},{7,6},{9,8},{11,10},{13,12},{15,14},{17,16},{19,... | collective-permute-start | bytes 2600 | tf_op jit(solution)/shard_map/ppermute | solution.py:35
  476.2 19.0 %collective-permute-start.35 = (f32[12,3,6,1]{0,3,2,1:T(1,128)S(1)}, f32[12,3,6,1]{0,3,2,1:T(1,128)S(1)}, u32[]{:S(2)}, u32[]{:S(2)}) collective-permute-start(f32[12,3,6,1]{0,3,2,1:T(1,128)S(1)} %get-tuple-element.3370), channel_id=1, source_target_pairs={{0,1},{2,3},{4,5},{6,7},{8,9},{10,11},{12,13},{14,15},{16,17},{18,... | collective-permute-start | bytes 2600 | tf_op jit(solution)/shard_map/ppermute | solution.py:34
  543.4 19.4 %collective-permute-start.42 = (f32[12,1,4,2]{0,3,2,1:T(2,128)S(1)}, f32[12,1,4,2]{0,3,2,1:T(2,128)S(1)}, u32[]{:S(2)}, u32[]{:S(2)}) collective-permute-start(f32[12,1,4,2]{0,3,2,1:T(2,128)S(1)} %bitcast.2249), channel_id=1, source_target_pairs={{8,0},{16,8},{24,16},{9,1},{17,9},{25,17},{10,2},{18,10},{26,18},{... | collective-permute-start | bytes 1160 | tf_op jit(solution)/shard_map/ppermute | solution.py:35
  544.7 18.1 %collective-permute-start.43 = (f32[12,1,4,2]{0,3,2,1:T(2,128)S(1)}, f32[12,1,4,2]{0,3,2,1:T(2,128)S(1)}, u32[]{:S(2)}, u32[]{:S(2)}) collective-permute-start(f32[12,1,4,2]{0,3,2,1:T(2,128)S(1)} %bitcast.2250), channel_id=1, source_target_pairs={{0,8},{8,16},{16,24},{1,9},{9,17},{17,25},{2,10},{10,18},{18,26},{... | collective-permute-start | bytes 1160 | tf_op jit(solution)/shard_map/ppermute | solution.py:34
  559.6 15.1 %collective-permute-start.48 = (f32[12,1,6,4]{0,3,2,1:T(4,128)S(1)}, f32[12,1,6,4]{0,3,2,1:T(4,128)S(1)}, u32[]{:S(2)}, u32[]{:S(2)}) collective-permute-start(f32[12,1,6,4]{0,3,2,1:T(4,128)S(1)} %get-tuple-element.3255), channel_id=1, source_target_pairs={{0,8},{8,16},{16,24},{1,9},{9,17},{17,25},{2,10},{10,18},{18,26},{... | collective-permute-start | bytes 3464 | tf_op jit(solution)/shard_map/ppermute | solution.py:34
  570.3 20.3 %collective-permute-start.46 = (f32[12,3,6,1]{0,3,2,1:T(1,128)S(1)}, f32[12,3,6,1]{0,3,2,1:T(1,128)S(1)}, u32[]{:S(2)}, u32[]{:S(2)}) collective-permute-start(f32[12,3,6,1]{0,3,2,1:T(1,128)S(1)} %get-tuple-element.3368), channel_id=1, source_target_pairs={{1,0},{3,2},{5,4},{7,6},{9,8},{11,10},{13,12},{15,14},{17,16},{19,... | collective-permute-start | bytes 2600 | tf_op jit(solution)/shard_map/ppermute | solution.py:35
  571.6 19.0 %collective-permute-start.47 = (f32[12,3,6,1]{0,3,2,1:T(1,128)S(1)}, f32[12,3,6,1]{0,3,2,1:T(1,128)S(1)}, u32[]{:S(2)}, u32[]{:S(2)}) collective-permute-start(f32[12,3,6,1]{0,3,2,1:T(1,128)S(1)} %get-tuple-element.3367), channel_id=1, source_target_pairs={{0,1},{2,3},{4,5},{6,7},{8,9},{10,11},{12,13},{14,15},{16,17},{18,... | collective-permute-start | bytes 2600 | tf_op jit(solution)/shard_map/ppermute | solution.py:34
  638.1 19.4 %collective-permute-start.54 = (f32[12,1,4,2]{0,3,2,1:T(2,128)S(1)}, f32[12,1,4,2]{0,3,2,1:T(2,128)S(1)}, u32[]{:S(2)}, u32[]{:S(2)}) collective-permute-start(f32[12,1,4,2]{0,3,2,1:T(2,128)S(1)} %bitcast.2260), channel_id=1, source_target_pairs={{8,0},{16,8},{24,16},{9,1},{17,9},{25,17},{10,2},{18,10},{26,18},{... | collective-permute-start | bytes 1160 | tf_op jit(solution)/shard_map/ppermute | solution.py:35
  639.4 18.1 %collective-permute-start.55 = (f32[12,1,4,2]{0,3,2,1:T(2,128)S(1)}, f32[12,1,4,2]{0,3,2,1:T(2,128)S(1)}, u32[]{:S(2)}, u32[]{:S(2)}) collective-permute-start(f32[12,1,4,2]{0,3,2,1:T(2,128)S(1)} %bitcast.2261), channel_id=1, source_target_pairs={{0,8},{8,16},{16,24},{1,9},{9,17},{17,25},{2,10},{10,18},{18,26},{... | collective-permute-start | bytes 1160 | tf_op jit(solution)/shard_map/ppermute | solution.py:34
  654.3 15.1 %collective-permute-start.60 = (f32[12,1,6,4]{0,3,2,1:T(4,128)S(1)}, f32[12,1,6,4]{0,3,2,1:T(4,128)S(1)}, u32[]{:S(2)}, u32[]{:S(2)}) collective-permute-start(f32[12,1,6,4]{0,3,2,1:T(4,128)S(1)} %get-tuple-element.3253), channel_id=1, source_target_pairs={{0,8},{8,16},{16,24},{1,9},{9,17},{17,25},{2,10},{10,18},{18,26},{... | collective-permute-start | bytes 3464 | tf_op jit(solution)/shard_map/ppermute | solution.py:34
  665.0 20.7 %collective-permute-start.58 = (f32[12,3,6,1]{0,3,2,1:T(1,128)S(1)}, f32[12,3,6,1]{0,3,2,1:T(1,128)S(1)}, u32[]{:S(2)}, u32[]{:S(2)}) collective-permute-start(f32[12,3,6,1]{0,3,2,1:T(1,128)S(1)} %get-tuple-element.3365), channel_id=1, source_target_pairs={{1,0},{3,2},{5,4},{7,6},{9,8},{11,10},{13,12},{15,14},{17,16},{19,... | collective-permute-start | bytes 2600 | tf_op jit(solution)/shard_map/ppermute | solution.py:35
  666.3 19.4 %collective-permute-start.59 = (f32[12,3,6,1]{0,3,2,1:T(1,128)S(1)}, f32[12,3,6,1]{0,3,2,1:T(1,128)S(1)}, u32[]{:S(2)}, u32[]{:S(2)}) collective-permute-start(f32[12,3,6,1]{0,3,2,1:T(1,128)S(1)} %get-tuple-element.3364), channel_id=1, source_target_pairs={{0,1},{2,3},{4,5},{6,7},{8,9},{10,11},{12,13},{14,15},{16,17},{18,... | collective-permute-start | bytes 2600 | tf_op jit(solution)/shard_map/ppermute | solution.py:34
  733.2 19.4 %collective-permute-start.66 = (f32[12,1,4,2]{0,3,2,1:T(2,128)S(1)}, f32[12,1,4,2]{0,3,2,1:T(2,128)S(1)}, u32[]{:S(2)}, u32[]{:S(2)}) collective-permute-start(f32[12,1,4,2]{0,3,2,1:T(2,128)S(1)} %bitcast.2271), channel_id=1, source_target_pairs={{8,0},{16,8},{24,16},{9,1},{17,9},{25,17},{10,2},{18,10},{26,18},{... | collective-permute-start | bytes 1160 | tf_op jit(solution)/shard_map/ppermute | solution.py:35
  734.5 18.1 %collective-permute-start.67 = (f32[12,1,4,2]{0,3,2,1:T(2,128)S(1)}, f32[12,1,4,2]{0,3,2,1:T(2,128)S(1)}, u32[]{:S(2)}, u32[]{:S(2)}) collective-permute-start(f32[12,1,4,2]{0,3,2,1:T(2,128)S(1)} %bitcast.2272), channel_id=1, source_target_pairs={{0,8},{8,16},{16,24},{1,9},{9,17},{17,25},{2,10},{10,18},{18,26},{... | collective-permute-start | bytes 1160 | tf_op jit(solution)/shard_map/ppermute | solution.py:34
  749.3 15.1 %collective-permute-start.72 = (f32[12,1,6,4]{0,3,2,1:T(4,128)S(1)}, f32[12,1,6,4]{0,3,2,1:T(4,128)S(1)}, u32[]{:S(2)}, u32[]{:S(2)}) collective-permute-start(f32[12,1,6,4]{0,3,2,1:T(4,128)S(1)} %get-tuple-element.3251), channel_id=1, source_target_pairs={{0,8},{8,16},{16,24},{1,9},{9,17},{17,25},{2,10},{10,18},{18,26},{... | collective-permute-start | bytes 3464 | tf_op jit(solution)/shard_map/ppermute | solution.py:34
  751.3 13.2 %collective-permute-start.73 = (f32[12,1,6,4]{0,3,2,1:T(4,128)S(1)}, f32[12,1,6,4]{0,3,2,1:T(4,128)S(1)}, u32[]{:S(2)}, u32[]{:S(2)}) collective-permute-start(f32[12,1,6,4]{0,3,2,1:T(4,128)S(1)} %get-tuple-element.3252), channel_id=1, source_target_pairs={{8,0},{16,8},{24,16},{9,1},{17,9},{25,17},{10,2},{18,10},{26,18},{... | collective-permute-start | bytes 3464 | tf_op jit(solution)/shard_map/ppermute | solution.py:35
  760.1 20.3 %collective-permute-start.70 = (f32[12,3,6,1]{0,3,2,1:T(1,128)S(1)}, f32[12,3,6,1]{0,3,2,1:T(1,128)S(1)}, u32[]{:S(2)}, u32[]{:S(2)}) collective-permute-start(f32[12,3,6,1]{0,3,2,1:T(1,128)S(1)} %get-tuple-element.3362), channel_id=1, source_target_pairs={{1,0},{3,2},{5,4},{7,6},{9,8},{11,10},{13,12},{15,14},{17,16},{19,... | collective-permute-start | bytes 2600 | tf_op jit(solution)/shard_map/ppermute | solution.py:35
  761.4 19.0 %collective-permute-start.71 = (f32[12,3,6,1]{0,3,2,1:T(1,128)S(1)}, f32[12,3,6,1]{0,3,2,1:T(1,128)S(1)}, u32[]{:S(2)}, u32[]{:S(2)}) collective-permute-start(f32[12,3,6,1]{0,3,2,1:T(1,128)S(1)} %get-tuple-element.3361), channel_id=1, source_target_pairs={{0,1},{2,3},{4,5},{6,7},{8,9},{10,11},{12,13},{14,15},{16,17},{18,... | collective-permute-start | bytes 2600 | tf_op jit(solution)/shard_map/ppermute | solution.py:34
  827.8 19.4 %collective-permute-start.78 = (f32[12,1,4,2]{0,3,2,1:T(2,128)S(1)}, f32[12,1,4,2]{0,3,2,1:T(2,128)S(1)}, u32[]{:S(2)}, u32[]{:S(2)}) collective-permute-start(f32[12,1,4,2]{0,3,2,1:T(2,128)S(1)} %bitcast.2282), channel_id=1, source_target_pairs={{8,0},{16,8},{24,16},{9,1},{17,9},{25,17},{10,2},{18,10},{26,18},{... | collective-permute-start | bytes 1160 | tf_op jit(solution)/shard_map/ppermute | solution.py:35
  829.1 18.1 %collective-permute-start.79 = (f32[12,1,4,2]{0,3,2,1:T(2,128)S(1)}, f32[12,1,4,2]{0,3,2,1:T(2,128)S(1)}, u32[]{:S(2)}, u32[]{:S(2)}) collective-permute-start(f32[12,1,4,2]{0,3,2,1:T(2,128)S(1)} %bitcast.2283), channel_id=1, source_target_pairs={{0,8},{8,16},{16,24},{1,9},{9,17},{17,25},{2,10},{10,18},{18,26},{... | collective-permute-start | bytes 1160 | tf_op jit(solution)/shard_map/ppermute | solution.py:34
  843.9 15.1 %collective-permute-start.84 = (f32[12,1,6,4]{0,3,2,1:T(4,128)S(1)}, f32[12,1,6,4]{0,3,2,1:T(4,128)S(1)}, u32[]{:S(2)}, u32[]{:S(2)}) collective-permute-start(f32[12,1,6,4]{0,3,2,1:T(4,128)S(1)} %get-tuple-element.3249), channel_id=1, source_target_pairs={{0,8},{8,16},{16,24},{1,9},{9,17},{17,25},{2,10},{10,18},{18,26},{... | collective-permute-start | bytes 3464 | tf_op jit(solution)/shard_map/ppermute | solution.py:34
  845.9 13.2 %collective-permute-start.85 = (f32[12,1,6,4]{0,3,2,1:T(4,128)S(1)}, f32[12,1,6,4]{0,3,2,1:T(4,128)S(1)}, u32[]{:S(2)}, u32[]{:S(2)}) collective-permute-start(f32[12,1,6,4]{0,3,2,1:T(4,128)S(1)} %get-tuple-element.3250), channel_id=1, source_target_pairs={{8,0},{16,8},{24,16},{9,1},{17,9},{25,17},{10,2},{18,10},{26,18},{... | collective-permute-start | bytes 3464 | tf_op jit(solution)/shard_map/ppermute | solution.py:35
  854.7 20.5 %collective-permute-start.82 = (f32[12,3,6,1]{0,3,2,1:T(1,128)S(1)}, f32[12,3,6,1]{0,3,2,1:T(1,128)S(1)}, u32[]{:S(2)}, u32[]{:S(2)}) collective-permute-start(f32[12,3,6,1]{0,3,2,1:T(1,128)S(1)} %get-tuple-element.3359), channel_id=1, source_target_pairs={{1,0},{3,2},{5,4},{7,6},{9,8},{11,10},{13,12},{15,14},{17,16},{19,... | collective-permute-start | bytes 2600 | tf_op jit(solution)/shard_map/ppermute | solution.py:35
  856.0 19.2 %collective-permute-start.83 = (f32[12,3,6,1]{0,3,2,1:T(1,128)S(1)}, f32[12,3,6,1]{0,3,2,1:T(1,128)S(1)}, u32[]{:S(2)}, u32[]{:S(2)}) collective-permute-start(f32[12,3,6,1]{0,3,2,1:T(1,128)S(1)} %get-tuple-element.3358), channel_id=1, source_target_pairs={{0,1},{2,3},{4,5},{6,7},{8,9},{10,11},{12,13},{14,15},{16,17},{18,... | collective-permute-start | bytes 2600 | tf_op jit(solution)/shard_map/ppermute | solution.py:34
  922.6 19.4 %collective-permute-start.90 = (f32[12,1,4,2]{0,3,2,1:T(2,128)S(1)}, f32[12,1,4,2]{0,3,2,1:T(2,128)S(1)}, u32[]{:S(2)}, u32[]{:S(2)}) collective-permute-start(f32[12,1,4,2]{0,3,2,1:T(2,128)S(1)} %bitcast.2293), channel_id=1, source_target_pairs={{8,0},{16,8},{24,16},{9,1},{17,9},{25,17},{10,2},{18,10},{26,18},{... | collective-permute-start | bytes 1160 | tf_op jit(solution)/shard_map/ppermute | solution.py:35
  923.9 18.1 %collective-permute-start.91 = (f32[12,1,4,2]{0,3,2,1:T(2,128)S(1)}, f32[12,1,4,2]{0,3,2,1:T(2,128)S(1)}, u32[]{:S(2)}, u32[]{:S(2)}) collective-permute-start(f32[12,1,4,2]{0,3,2,1:T(2,128)S(1)} %bitcast.2294), channel_id=1, source_target_pairs={{0,8},{8,16},{16,24},{1,9},{9,17},{17,25},{2,10},{10,18},{18,26},{... | collective-permute-start | bytes 1160 | tf_op jit(solution)/shard_map/ppermute | solution.py:34
  938.7 15.1 %collective-permute-start.96 = (f32[12,1,6,4]{0,3,2,1:T(4,128)S(1)}, f32[12,1,6,4]{0,3,2,1:T(4,128)S(1)}, u32[]{:S(2)}, u32[]{:S(2)}) collective-permute-start(f32[12,1,6,4]{0,3,2,1:T(4,128)S(1)} %get-tuple-element.3247), channel_id=1, source_target_pairs={{0,8},{8,16},{16,24},{1,9},{9,17},{17,25},{2,10},{10,18},{18,26},{... | collective-permute-start | bytes 3464 | tf_op jit(solution)/shard_map/ppermute | solution.py:34
  949.5 20.3 %collective-permute-start.94 = (f32[12,3,6,1]{0,3,2,1:T(1,128)S(1)}, f32[12,3,6,1]{0,3,2,1:T(1,128)S(1)}, u32[]{:S(2)}, u32[]{:S(2)}) collective-permute-start(f32[12,3,6,1]{0,3,2,1:T(1,128)S(1)} %get-tuple-element.3356), channel_id=1, source_target_pairs={{1,0},{3,2},{5,4},{7,6},{9,8},{11,10},{13,12},{15,14},{17,16},{19,... | collective-permute-start | bytes 2600 | tf_op jit(solution)/shard_map/ppermute | solution.py:35
  950.8 19.0 %collective-permute-start.95 = (f32[12,3,6,1]{0,3,2,1:T(1,128)S(1)}, f32[12,3,6,1]{0,3,2,1:T(1,128)S(1)}, u32[]{:S(2)}, u32[]{:S(2)}) collective-permute-start(f32[12,3,6,1]{0,3,2,1:T(1,128)S(1)} %get-tuple-element.3355), channel_id=1, source_target_pairs={{0,1},{2,3},{4,5},{6,7},{8,9},{10,11},{12,13},{14,15},{16,17},{18,... | collective-permute-start | bytes 2600 | tf_op jit(solution)/shard_map/ppermute | solution.py:34
  1017.2 19.4 %collective-permute-start.102 = (f32[12,1,4,2]{0,3,2,1:T(2,128)S(1)}, f32[12,1,4,2]{0,3,2,1:T(2,128)S(1)}, u32[]{:S(2)}, u32[]{:S(2)}) collective-permute-start(f32[12,1,4,2]{0,3,2,1:T(2,128)S(1)} %bitcast.2304), channel_id=1, source_target_pairs={{8,0},{16,8},{24,16},{9,1},{17,9},{25,17},{10,2},{18,10},{26,18},{... | collective-permute-start | bytes 1160 | tf_op jit(solution)/shard_map/ppermute | solution.py:35
  1018.5 18.1 %collective-permute-start.103 = (f32[12,1,4,2]{0,3,2,1:T(2,128)S(1)}, f32[12,1,4,2]{0,3,2,1:T(2,128)S(1)}, u32[]{:S(2)}, u32[]{:S(2)}) collective-permute-start(f32[12,1,4,2]{0,3,2,1:T(2,128)S(1)} %bitcast.2305), channel_id=1, source_target_pairs={{0,8},{8,16},{16,24},{1,9},{9,17},{17,25},{2,10},{10,18},{18,26},{... | collective-permute-start | bytes 1160 | tf_op jit(solution)/shard_map/ppermute | solution.py:34
  1033.4 15.1 %collective-permute-start.108 = (f32[12,1,6,4]{0,3,2,1:T(4,128)S(1)}, f32[12,1,6,4]{0,3,2,1:T(4,128)S(1)}, u32[]{:S(2)}, u32[]{:S(2)}) collective-permute-start(f32[12,1,6,4]{0,3,2,1:T(4,128)S(1)} %get-tuple-element.3245), channel_id=1, source_target_pairs={{0,8},{8,16},{16,24},{1,9},{9,17},{17,25},{2,10},{10,18},{18,26},{... | collective-permute-start | bytes 3464 | tf_op jit(solution)/shard_map/ppermute | solution.py:34
  1035.3 13.2 %collective-permute-start.109 = (f32[12,1,6,4]{0,3,2,1:T(4,128)S(1)}, f32[12,1,6,4]{0,3,2,1:T(4,128)S(1)}, u32[]{:S(2)}, u32[]{:S(2)}) collective-permute-start(f32[12,1,6,4]{0,3,2,1:T(4,128)S(1)} %get-tuple-element.3246), channel_id=1, source_target_pairs={{8,0},{16,8},{24,16},{9,1},{17,9},{25,17},{10,2},{18,10},{26,18},{... | collective-permute-start | bytes 3464 | tf_op jit(solution)/shard_map/ppermute | solution.py:35
  1044.1 20.5 %collective-permute-start.106 = (f32[12,3,6,1]{0,3,2,1:T(1,128)S(1)}, f32[12,3,6,1]{0,3,2,1:T(1,128)S(1)}, u32[]{:S(2)}, u32[]{:S(2)}) collective-permute-start(f32[12,3,6,1]{0,3,2,1:T(1,128)S(1)} %get-tuple-element.3353), channel_id=1, source_target_pairs={{1,0},{3,2},{5,4},{7,6},{9,8},{11,10},{13,12},{15,14},{17,16},{19,... | collective-permute-start | bytes 2600 | tf_op jit(solution)/shard_map/ppermute | solution.py:35
  1045.4 19.2 %collective-permute-start.107 = (f32[12,3,6,1]{0,3,2,1:T(1,128)S(1)}, f32[12,3,6,1]{0,3,2,1:T(1,128)S(1)}, u32[]{:S(2)}, u32[]{:S(2)}) collective-permute-start(f32[12,3,6,1]{0,3,2,1:T(1,128)S(1)} %get-tuple-element.3352), channel_id=1, source_target_pairs={{0,1},{2,3},{4,5},{6,7},{8,9},{10,11},{12,13},{14,15},{16,17},{18,... | collective-permute-start | bytes 2600 | tf_op jit(solution)/shard_map/ppermute | solution.py:34
  1112.0 19.4 %collective-permute-start.114 = (f32[12,1,4,2]{0,3,2,1:T(2,128)S(1)}, f32[12,1,4,2]{0,3,2,1:T(2,128)S(1)}, u32[]{:S(2)}, u32[]{:S(2)}) collective-permute-start(f32[12,1,4,2]{0,3,2,1:T(2,128)S(1)} %bitcast.2315), channel_id=1, source_target_pairs={{8,0},{16,8},{24,16},{9,1},{17,9},{25,17},{10,2},{18,10},{26,18},{... | collective-permute-start | bytes 1160 | tf_op jit(solution)/shard_map/ppermute | solution.py:35
  1113.3 18.1 %collective-permute-start.115 = (f32[12,1,4,2]{0,3,2,1:T(2,128)S(1)}, f32[12,1,4,2]{0,3,2,1:T(2,128)S(1)}, u32[]{:S(2)}, u32[]{:S(2)}) collective-permute-start(f32[12,1,4,2]{0,3,2,1:T(2,128)S(1)} %bitcast.2316), channel_id=1, source_target_pairs={{0,8},{8,16},{16,24},{1,9},{9,17},{17,25},{2,10},{10,18},{18,26},{... | collective-permute-start | bytes 1160 | tf_op jit(solution)/shard_map/ppermute | solution.py:34
  1128.2 15.1 %collective-permute-start.120 = (f32[12,1,6,4]{0,3,2,1:T(4,128)S(1)}, f32[12,1,6,4]{0,3,2,1:T(4,128)S(1)}, u32[]{:S(2)}, u32[]{:S(2)}) collective-permute-start(f32[12,1,6,4]{0,3,2,1:T(4,128)S(1)} %get-tuple-element.3243), channel_id=1, source_target_pairs={{0,8},{8,16},{16,24},{1,9},{9,17},{17,25},{2,10},{10,18},{18,26},{... | collective-permute-start | bytes 3464 | tf_op jit(solution)/shard_map/ppermute | solution.py:34
  1138.9 20.3 %collective-permute-start.118 = (f32[12,3,6,1]{0,3,2,1:T(1,128)S(1)}, f32[12,3,6,1]{0,3,2,1:T(1,128)S(1)}, u32[]{:S(2)}, u32[]{:S(2)}) collective-permute-start(f32[12,3,6,1]{0,3,2,1:T(1,128)S(1)} %get-tuple-element.3350), channel_id=1, source_target_pairs={{1,0},{3,2},{5,4},{7,6},{9,8},{11,10},{13,12},{15,14},{17,16},{19,... | collective-permute-start | bytes 2600 | tf_op jit(solution)/shard_map/ppermute | solution.py:35
  1140.2 19.0 %collective-permute-start.119 = (f32[12,3,6,1]{0,3,2,1:T(1,128)S(1)}, f32[12,3,6,1]{0,3,2,1:T(1,128)S(1)}, u32[]{:S(2)}, u32[]{:S(2)}) collective-permute-start(f32[12,3,6,1]{0,3,2,1:T(1,128)S(1)} %get-tuple-element.3349), channel_id=1, source_target_pairs={{0,1},{2,3},{4,5},{6,7},{8,9},{10,11},{12,13},{14,15},{16,17},{18,... | collective-permute-start | bytes 2600 | tf_op jit(solution)/shard_map/ppermute | solution.py:34
  1206.6 19.4 %collective-permute-start.126 = (f32[12,1,4,2]{0,3,2,1:T(2,128)S(1)}, f32[12,1,4,2]{0,3,2,1:T(2,128)S(1)}, u32[]{:S(2)}, u32[]{:S(2)}) collective-permute-start(f32[12,1,4,2]{0,3,2,1:T(2,128)S(1)} %bitcast.2326), channel_id=1, source_target_pairs={{8,0},{16,8},{24,16},{9,1},{17,9},{25,17},{10,2},{18,10},{26,18},{... | collective-permute-start | bytes 1160 | tf_op jit(solution)/shard_map/ppermute | solution.py:35
  1207.9 18.1 %collective-permute-start.127 = (f32[12,1,4,2]{0,3,2,1:T(2,128)S(1)}, f32[12,1,4,2]{0,3,2,1:T(2,128)S(1)}, u32[]{:S(2)}, u32[]{:S(2)}) collective-permute-start(f32[12,1,4,2]{0,3,2,1:T(2,128)S(1)} %bitcast.2327), channel_id=1, source_target_pairs={{0,8},{8,16},{16,24},{1,9},{9,17},{17,25},{2,10},{10,18},{18,26},{... | collective-permute-start | bytes 1160 | tf_op jit(solution)/shard_map/ppermute | solution.py:34
  1222.8 15.1 %collective-permute-start.132 = (f32[12,1,6,4]{0,3,2,1:T(4,128)S(1)}, f32[12,1,6,4]{0,3,2,1:T(4,128)S(1)}, u32[]{:S(2)}, u32[]{:S(2)}) collective-permute-start(f32[12,1,6,4]{0,3,2,1:T(4,128)S(1)} %get-tuple-element.3241), channel_id=1, source_target_pairs={{0,8},{8,16},{16,24},{1,9},{9,17},{17,25},{2,10},{10,18},{18,26},{... | collective-permute-start | bytes 3464 | tf_op jit(solution)/shard_map/ppermute | solution.py:34
  1224.7 13.2 %collective-permute-start.133 = (f32[12,1,6,4]{0,3,2,1:T(4,128)S(1)}, f32[12,1,6,4]{0,3,2,1:T(4,128)S(1)}, u32[]{:S(2)}, u32[]{:S(2)}) collective-permute-start(f32[12,1,6,4]{0,3,2,1:T(4,128)S(1)} %get-tuple-element.3242), channel_id=1, source_target_pairs={{8,0},{16,8},{24,16},{9,1},{17,9},{25,17},{10,2},{18,10},{26,18},{... | collective-permute-start | bytes 3464 | tf_op jit(solution)/shard_map/ppermute | solution.py:35
  1233.5 20.3 %collective-permute-start.130 = (f32[12,3,6,1]{0,3,2,1:T(1,128)S(1)}, f32[12,3,6,1]{0,3,2,1:T(1,128)S(1)}, u32[]{:S(2)}, u32[]{:S(2)}) collective-permute-start(f32[12,3,6,1]{0,3,2,1:T(1,128)S(1)} %get-tuple-element.3347), channel_id=1, source_target_pairs={{1,0},{3,2},{5,4},{7,6},{9,8},{11,10},{13,12},{15,14},{17,16},{19,... | collective-permute-start | bytes 2600 | tf_op jit(solution)/shard_map/ppermute | solution.py:35
  1234.8 19.0 %collective-permute-start.131 = (f32[12,3,6,1]{0,3,2,1:T(1,128)S(1)}, f32[12,3,6,1]{0,3,2,1:T(1,128)S(1)}, u32[]{:S(2)}, u32[]{:S(2)}) collective-permute-start(f32[12,3,6,1]{0,3,2,1:T(1,128)S(1)} %get-tuple-element.3346), channel_id=1, source_target_pairs={{0,1},{2,3},{4,5},{6,7},{8,9},{10,11},{12,13},{14,15},{16,17},{18,... | collective-permute-start | bytes 2600 | tf_op jit(solution)/shard_map/ppermute | solution.py:34
  (261 other events, 2457.2 us)
where the time goes:
time: 1320 us; the launch traced here: 1300 us
  blocking collectives  416 us (32%)
  starting transfers between devices  329 us (25%)
  local copies, waits for them, and re-layouts  174 us (13%)
  matrix products  170 us (13%)
  waiting for transfers between devices  92.3 us (7%)
  other arithmetic  75 us (6%)
  between operations  46.2 us (4%)
    psum x10, blocking collectives, both_products(): lax.psum((jnp.sum(residual * scaled), jnp.sum(image * scaled)), ('gx', 'g...  416 us
    ppermute x69, starting transfers between devices, padded(): before = lax.ppermute(last, axis, up)  240 us
    ppermute x69, starting transfers between devices, padded(): after = lax.ppermute(first, axis, down)  89.3 us
    ppermute x69, waiting for transfers between devices, padded(): after = lax.ppermute(first, axis, down)  79.4 us
    dot_general x10, matrix products, operate(): sent = jnp.einsum('dbaxyz,bxyz->daxyz', coupling, vector, precision=exact)  56.8 us
    another operation x65, local copies, waits for them, and re-layouts  28.1 us
  transfers between devices with their start and end apart: 138, of which 33 were waited for; matrix products, arithmetic and copies ran while one was open for 22% of the time, Pallas kernels for 0%

commit v1 on v0

--- a/solution.py
+++ b/solution.py
@@ -24,6 +24,12 @@
 )
 
 
+def meshes_start(z):
+    for jj in (("gy", "gz"), "gx"):
+        z = lax.psum(z, jj)
+    return z
+
+
 def padded(value, sides, width):
     for axis, dim in sides:
         devices, length = (lax.axis_size(axis), value.shape[dim])
@@ -119,7 +125,7 @@
 
 
 def both_products(residual, scaled, image):
-    return lax.psum((jnp.sum(residual * scaled), jnp.sum(image * scaled)), ("gx", "gy", "gz"))
+    return meshes_start((jnp.sum(residual * scaled), jnp.sum(image * scaled)))
 
 
 def on_device(source_points, target_points, normals, weights, blocks, affines, anchor):

time: 1320 us -> 1140 us (0.86)
  blocking collectives: 416 us -> 247 us
    psum x10 -> x20, blocking collectives: 416 us -> 247 us  [meshes_start(): z = lax.psum(z, jj)]
  transfers between devices with their start and end apart: 138 -> 138, of which waited for: 33 -> 33; matrix products, arithmetic and copies ran while one was open for 22% -> 25% of each run, Pallas kernels for 0% -> 0%
where the time goes in v1:
time: 1140 us; the launch traced here: 1120 us
  starting transfers between devices  329 us (29%)
  blocking collectives  247 us (22%)
  local copies, waits for them, and re-layouts  173 us (15%)
  matrix products  160 us (14%)
  waiting for transfers between devices  92.3 us (8%)
  other arithmetic  74.3 us (7%)
  between operations  47.6 us (4%)
    psum x20, blocking collectives, meshes_start(): z = lax.psum(z, jj)  247 us
    ppermute x69, starting transfers between devices, padded(): before = lax.ppermute(last, axis, up)  239 us
    ppermute x69, starting transfers between devices, padded(): after = lax.ppermute(first, axis, down)  89.3 us
    ppermute x69, waiting for transfers between devices, padded(): after = lax.ppermute(first, axis, down)  79.3 us
    dot_general x10, matrix products, operate(): sent = jnp.einsum('dbaxyz,bxyz->daxyz', coupling, vector, precision=exact)  56.8 us
    another operation x65, local copies, waits for them, and re-layouts  28.1 us
    dot_general x26, matrix products, mapped(): jnp.einsum('cexyz,exyzp->cxyzp', matrix, lifted_points, precision=lax.Pre...  24.5 us
  transfers between devices with their start and end apart: 138, of which 33 were waited for; matrix products, arithmetic and copies ran while one was open for 25% of the time, Pallas kernels for 0%

profile of v1, /device:TPU:0, one launch (start us, length us, event | category | flops | bytes accessed | tf_op | source)
XLA Modules:
  0.0 1122.0 jit_solution(4736576652661493938)
XLA Ops:
  0.6 5.1 collective-permute-start
  7.8 5.1 collective-permute-start.6
  162.4 5.5 pad_maximum_fusion
  318.2 4.6 collective-permute-start.14
  345.2 5.1 collective-permute-start.19
  350.7 5.7 fusion.452
  367.4 4.5 collective-permute-start.21
  383.4 5.3 collective-permute-done.27
  394.9 12.6 %all-reduce.46 = (f32[]{:T(128)}, f32[]{:T(128)}) all-reduce(f32[]{:T(128)} %get-tuple-element.2981, f32[]{:T(128)} %get-tuple-element.2980), channel_id=1, replica_groups=mesh['gx'=4,'gy'=4,'gz'=2] {'gy','gz'}, use_global_device_ids=true, to_apply=%region_14.0 | all-reduce | flops 2 | bytes 16 | tf_op jit(solution)/shard_map/psum | solution.py:29
  407.5 11.6 %all-reduce.56 = (f32[]{:T(128)}, f32[]{:T(128)}) all-reduce(f32[]{:T(128)} %get-tuple-element.3000, f32[]{:T(128)} %get-tuple-element.3001), channel_id=1, replica_groups=mesh['gx'=4,'gy'=4,'gz'=2] {'gx'}, use_global_device_ids=true, to_apply=%region_15.0 | all-reduce | flops 2 | bytes 16 | tf_op jit(solution)/shard_map/psum | solution.py:29
  422.0 4.5 collective-permute-start.31
  426.8 5.7 fusion.446
  441.4 4.5 collective-permute-start.33
  451.7 5.3 collective-permute-start.38
  458.4 5.3 collective-permute-done.39
  470.2 13.1 %all-reduce.45 = (f32[]{:T(128)}, f32[]{:T(128)}) all-reduce(f32[]{:T(128)} %get-tuple-element.2979, f32[]{:T(128)} %get-tuple-element.2978), channel_id=1, replica_groups=mesh['gx'=4,'gy'=4,'gz'=2] {'gy','gz'}, use_global_device_ids=true, to_apply=%region_20.0 | all-reduce | flops 2 | bytes 16 | tf_op jit(solution)/shard_map/psum | solution.py:29
  483.3 11.7 %all-reduce.55 = (f32[]{:T(128)}, f32[]{:T(128)}) all-reduce(f32[]{:T(128)} %get-tuple-element.2998, f32[]{:T(128)} %get-tuple-element.2999), channel_id=1, replica_groups=mesh['gx'=4,'gy'=4,'gz'=2] {'gx'}, use_global_device_ids=true, to_apply=%region_21.0 | all-reduce | flops 2 | bytes 16 | tf_op jit(solution)/shard_map/psum | solution.py:29
  501.1 4.5 collective-permute-start.43
  505.9 5.7 fusion.440
  520.4 4.5 collective-permute-start.45
  530.7 4.9 collective-permute-start.50
  536.9 5.3 collective-permute-done.51
  548.4 13.0 %all-reduce.44 = (f32[]{:T(128)}, f32[]{:T(128)}) all-reduce(f32[]{:T(128)} %get-tuple-element.2977, f32[]{:T(128)} %get-tuple-element.2976), channel_id=1, replica_groups=mesh['gx'=4,'gy'=4,'gz'=2] {'gy','gz'}, use_global_device_ids=true, to_apply=%region_26.0 | all-reduce | flops 2 | bytes 16 | tf_op jit(solution)/shard_map/psum | solution.py:29
  561.5 11.6 %all-reduce.54 = (f32[]{:T(128)}, f32[]{:T(128)}) all-reduce(f32[]{:T(128)} %get-tuple-element.2996, f32[]{:T(128)} %get-tuple-element.2997), channel_id=1, replica_groups=mesh['gx'=4,'gy'=4,'gz'=2] {'gx'}, use_global_device_ids=true, to_apply=%region_27.0 | all-reduce | flops 2 | bytes 16 | tf_op jit(solution)/shard_map/psum | solution.py:29
  578.7 4.5 collective-permute-start.55
  583.4 5.7 fusion.434
  608.3 4.9 collective-permute-start.62
  614.5 5.3 collective-permute-done.63
  626.0 13.1 %all-reduce.43 = (f32[]{:T(128)}, f32[]{:T(128)}) all-reduce(f32[]{:T(128)} %get-tuple-element.2975, f32[]{:T(128)} %get-tuple-element.2974), channel_id=1, replica_groups=mesh['gx'=4,'gy'=4,'gz'=2] {'gy','gz'}, use_global_device_ids=true, to_apply=%region_32.0 | all-reduce | flops 2 | bytes 16 | tf_op jit(solution)/shard_map/psum | solution.py:29
  639.1 11.7 %all-reduce.53 = (f32[]{:T(128)}, f32[]{:T(128)}) all-reduce(f32[]{:T(128)} %get-tuple-element.2994, f32[]{:T(128)} %get-tuple-element.2995), channel_id=1, replica_groups=mesh['gx'=4,'gy'=4,'gz'=2] {'gx'}, use_global_device_ids=true, to_apply=%region_33.0 | all-reduce | flops 2 | bytes 16 | tf_op jit(solution)/shard_map/psum | solution.py:29
  656.3 4.8 collective-permute-start.67
  661.2 5.7 fusion.428
  686.1 4.9 collective-permute-start.74
  692.3 5.3 collective-permute-done.75
  703.8 13.0 %all-reduce.42 = (f32[]{:T(128)}, f32[]{:T(128)}) all-reduce(f32[]{:T(128)} %get-tuple-element.2973, f32[]{:T(128)} %get-tuple-element.2972), channel_id=1, replica_groups=mesh['gx'=4,'gy'=4,'gz'=2] {'gy','gz'}, use_global_device_ids=true, to_apply=%region_38.0 | all-reduce | flops 2 | bytes 16 | tf_op jit(solution)/shard_map/psum | solution.py:29
  716.8 11.6 %all-reduce.52 = (f32[]{:T(128)}, f32[]{:T(128)}) all-reduce(f32[]{:T(128)} %get-tuple-element.2992, f32[]{:T(128)} %get-tuple-element.2993), channel_id=1, replica_groups=mesh['gx'=4,'gy'=4,'gz'=2] {'gx'}, use_global_device_ids=true, to_apply=%region_39.0 | all-reduce | flops 2 | bytes 16 | tf_op jit(solution)/shard_map/psum | solution.py:29
  738.7 5.7 fusion.422
  763.5 4.9 collective-permute-start.86
  769.7 5.3 collective-permute-done.87
  781.3 13.1 %all-reduce.41 = (f32[]{:T(128)}, f32[]{:T(128)}) all-reduce(f32[]{:T(128)} %get-tuple-element.2971, f32[]{:T(128)} %get-tuple-element.2970), channel_id=1, replica_groups=mesh['gx'=4,'gy'=4,'gz'=2] {'gy','gz'}, use_global_device_ids=true, to_apply=%region_44.0 | all-reduce | flops 2 | bytes 16 | tf_op jit(solution)/shard_map/psum | solution.py:29
  794.4 11.7 %all-reduce.51 = (f32[]{:T(128)}, f32[]{:T(128)}) all-reduce(f32[]{:T(128)} %get-tuple-element.2990, f32[]{:T(128)} %get-tuple-element.2991), channel_id=1, replica_groups=mesh['gx'=4,'gy'=4,'gz'=2] {'gx'}, use_global_device_ids=true, to_apply=%region_45.0 | all-reduce | flops 2 | bytes 16 | tf_op jit(solution)/shard_map/psum | solution.py:29
  811.5 5.0 collective-permute-start.91
  816.7 5.7 fusion.416
  831.2 4.5 collective-permute-start.93
  841.5 4.9 collective-permute-start.98
  847.7 5.3 collective-permute-done.99
  859.2 13.0 %all-reduce.40 = (f32[]{:T(128)}, f32[]{:T(128)}) all-reduce(f32[]{:T(128)} %get-tuple-element.2969, f32[]{:T(128)} %get-tuple-element.2968), channel_id=1, replica_groups=mesh['gx'=4,'gy'=4,'gz'=2] {'gy','gz'}, use_global_device_ids=true, to_apply=%region_50.0 | all-reduce | flops 2 | bytes 16 | tf_op jit(solution)/shard_map/psum | solution.py:29
  872.3 11.6 %all-reduce.50 = (f32[]{:T(128)}, f32[]{:T(128)}) all-reduce(f32[]{:T(128)} %get-tuple-element.2988, f32[]{:T(128)} %get-tuple-element.2989), channel_id=1, replica_groups=mesh['gx'=4,'gy'=4,'gz'=2] {'gx'}, use_global_device_ids=true, to_apply=%region_51.0 | all-reduce | flops 2 | bytes 16 | tf_op jit(solution)/shard_map/psum | solution.py:29
  894.1 5.7 fusion.410
  918.9 4.9 collective-permute-start.110
  925.2 5.3 collective-permute-done.111
  936.7 13.1 %all-reduce.39 = (f32[]{:T(128)}, f32[]{:T(128)}) all-reduce(f32[]{:T(128)} %get-tuple-element.2967, f32[]{:T(128)} %get-tuple-element.2966), channel_id=1, replica_groups=mesh['gx'=4,'gy'=4,'gz'=2] {'gy','gz'}, use_global_device_ids=true, to_apply=%region_56.0 | all-reduce | flops 2 | bytes 16 | tf_op jit(solution)/shard_map/psum | solution.py:29
  949.8 11.7 %all-reduce.49 = (f32[]{:T(128)}, f32[]{:T(128)}) all-reduce(f32[]{:T(128)} %get-tuple-element.2986, f32[]{:T(128)} %get-tuple-element.2987), channel_id=1, replica_groups=mesh['gx'=4,'gy'=4,'gz'=2] {'gx'}, use_global_device_ids=true, to_apply=%region_57.0 | all-reduce | flops 2 | bytes 16 | tf_op jit(solution)/shard_map/psum | solution.py:29
  966.9 4.7 collective-permute-start.115
  971.9 5.7 fusion.404
  996.7 4.9 collective-permute-start.122
  1002.9 5.3 collective-permute-done.123
  1014.4 13.0 %all-reduce.38 = (f32[]{:T(128)}, f32[]{:T(128)}) all-reduce(f32[]{:T(128)} %get-tuple-element.2965, f32[]{:T(128)} %get-tuple-element.2964), channel_id=1, replica_groups=mesh['gx'=4,'gy'=4,'gz'=2] {'gy','gz'}, use_global_device_ids=true, to_apply=%region_62.0 | all-reduce | flops 2 | bytes 16 | tf_op jit(solution)/shard_map/psum | solution.py:29
  1027.5 11.6 %all-reduce.48 = (f32[]{:T(128)}, f32[]{:T(128)}) all-reduce(f32[]{:T(128)} %get-tuple-element.2984, f32[]{:T(128)} %get-tuple-element.2985), channel_id=1, replica_groups=mesh['gx'=4,'gy'=4,'gz'=2] {'gx'}, use_global_device_ids=true, to_apply=%region_63.0 | all-reduce | flops 2 | bytes 16 | tf_op jit(solution)/shard_map/psum | solution.py:29
  1049.3 5.7 fusion.398
  1074.1 4.9 collective-permute-start.134
  1080.4 5.3 collective-permute-done.135
  1091.9 13.1 %all-reduce.37 = (f32[]{:T(128)}, f32[]{:T(128)}) all-reduce(f32[]{:T(128)} %get-tuple-element.2963, f32[]{:T(128)} %get-tuple-element.2962), channel_id=1, replica_groups=mesh['gx'=4,'gy'=4,'gz'=2] {'gy','gz'}, use_global_device_ids=true, to_apply=%region_68.0 | all-reduce | flops 2 | bytes 16 | tf_op jit(solution)/shard_map/psum | solution.py:29
  1105.0 11.7 %all-reduce.47 = (f32[]{:T(128)}, f32[]{:T(128)}) all-reduce(f32[]{:T(128)} %get-tuple-element.2982, f32[]{:T(128)} %get-tuple-element.2983), channel_id=1, replica_groups=mesh['gx'=4,'gy'=4,'gz'=2] {'gx'}, use_global_device_ids=true, to_apply=%region_69.0 | all-reduce | flops 2 | bytes 16 | tf_op jit(solution)/shard_map/psum | solution.py:29
  (1684 shorter events, 601.8 us)
Async XLA Ops:
  0.6 51.9 %collective-permute-start = (f32[39,1,4,2,512]{4,3,2,1,0:T(2,128)}, f32[39,1,4,2,512]{4,3,2,1,0:T(2,128)S(1)}, u32[]{:S(2)}, u32[]{:S(2)}) collective-permute-start(f32[39,1,4,2,512]{4,3,2,1,0:T(2,128)} %bitcast.2152), channel_id=1, source_target_pairs={{0,8},{8,16},{16,24},{1,9},{9,17},{17,25},{2,10},{10,18},{18,26},{... | collective-permute-start | bytes 1916936 | tf_op jit(solution)/shard_map/ppermute | solution.py:40
  5.8 46.8 %collective-permute-start.1 = (f32[39,1,4,2,512]{4,3,2,1,0:T(2,128)}, f32[39,1,4,2,512]{4,3,2,1,0:T(2,128)S(1)}, u32[]{:S(2)}, u32[]{:S(2)}) collective-permute-start(f32[39,1,4,2,512]{4,3,2,1,0:T(2,128)} %bitcast.2153), channel_id=1, source_target_pairs={{8,0},{16,8},{24,16},{9,1},{17,9},{25,17},{10,2},{18,10},{26,18},{... | collective-permute-start | bytes 1916936 | tf_op jit(solution)/shard_map/ppermute | solution.py:41
  7.8 124.2 %collective-permute-start.6 = (f32[12,1,4,2,1]{0,2,4,3,1:T(4,128)S(1)}, f32[12,1,4,2,1]{0,2,4,3,1:T(4,128)}, u32[]{:S(2)}, u32[]{:S(2)}) collective-permute-start(f32[12,1,4,2,1]{0,2,4,3,1:T(4,128)S(1)} %bitcast.2434), channel_id=1, source_target_pairs={{0,8},{8,16},{16,24},{1,9},{9,17},{17,25},{2,10},{10,18},{18,26},{... | collective-permute-start | bytes 1160 | tf_op jit(solution)/shard_map/ppermute | solution.py:40
  12.9 119.0 %collective-permute-start.7 = (f32[12,1,4,2,1]{0,2,4,3,1:T(4,128)S(1)}, f32[12,1,4,2,1]{0,2,4,3,1:T(4,128)}, u32[]{:S(2)}, u32[]{:S(2)}) collective-permute-start(f32[12,1,4,2,1]{0,2,4,3,1:T(4,128)S(1)} %bitcast.2435), channel_id=1, source_target_pairs={{8,0},{16,8},{24,16},{9,1},{17,9},{25,17},{10,2},{18,10},{26,18},{... | collective-permute-start | bytes 1160 | tf_op jit(solution)/shard_map/ppermute | solution.py:41
  53.9 64.6 %collective-permute-start.2 = (f32[39,3,1,2,512]{4,3,2,1,0:T(2,128)}, f32[39,3,1,2,512]{4,3,2,1,0:T(2,128)S(1)}, u32[]{:S(2)}, u32[]{:S(2)}) collective-permute-start(f32[39,3,1,2,512]{4,3,2,1,0:T(2,128)} %get-tuple-element.3050), channel_id=1, source_target_pairs={{0,2},{2,4},{4,6},{1,3},{3,5},{5,7},{8,10},{10,12},{12,14},{9,11},... | collective-permute-start | bytes 1437704 | tf_op jit(solution)/shard_map/ppermute | solution.py:40
  57.4 61.1 %collective-permute-start.3 = (f32[39,3,1,2,512]{4,3,2,1,0:T(2,128)}, f32[39,3,1,2,512]{4,3,2,1,0:T(2,128)S(1)}, u32[]{:S(2)}, u32[]{:S(2)}) collective-permute-start(f32[39,3,1,2,512]{4,3,2,1,0:T(2,128)} %get-tuple-element.3051), channel_id=1, source_target_pairs={{2,0},{4,2},{6,4},{3,1},{5,3},{7,5},{10,8},{12,10},{14,12},{11,9},... | collective-permute-start | bytes 1437704 | tf_op jit(solution)/shard_map/ppermute | solution.py:41
  124.0 38.5 %collective-permute-start.4 = (f32[39,3,6,1,512]{4,3,2,1,0:T(1,128)}, f32[39,3,6,1,512]{4,3,2,1,0:T(1,128)}, u32[]{:S(2)}, u32[]{:S(2)}) collective-permute-start(f32[39,3,6,1,512]{4,3,2,1,0:T(1,128)} %get-tuple-element.3048), channel_id=1, source_target_pairs={{0,1},{2,3},{4,5},{6,7},{8,9},{10,11},{12,13},{14,15},{16,17},{18,... | collective-permute-start | bytes 4313096 | tf_op jit(solution)/shard_map/ppermute | solution.py:40
  126.4 36.1 %collective-permute-start.5 = (f32[39,3,6,1,512]{4,3,2,1,0:T(1,128)}, f32[39,3,6,1,512]{4,3,2,1,0:T(1,128)}, u32[]{:S(2)}, u32[]{:S(2)}) collective-permute-start(f32[39,3,6,1,512]{4,3,2,1,0:T(1,128)} %get-tuple-element.3049), channel_id=1, source_target_pairs={{1,0},{3,2},{5,4},{7,6},{9,8},{11,10},{13,12},{15,14},{17,16},{19,... | collective-permute-start | bytes 4313096 | tf_op jit(solution)/shard_map/ppermute | solution.py:41
  266.7 50.7 %collective-permute-start.12 = (f32[156,1,6,4]{0,3,2,1:T(4,128)S(1)}, f32[156,1,6,4]{0,3,2,1:T(4,128)S(1)}, u32[]{:S(2)}, u32[]{:S(2)}) collective-permute-start(f32[156,1,6,4]{0,3,2,1:T(4,128)S(1)} %get-tuple-element.3090), channel_id=1, source_target_pairs={{0,8},{8,16},{16,24},{1,9},{9,17},{17,25},{2,10},{10,18},{18,26},{... | collective-permute-start | bytes 44936 | tf_op jit(solution)/shard_map/ppermute | solution.py:40
  271.2 46.2 %collective-permute-start.13 = (f32[156,1,6,4]{0,3,2,1:T(4,128)S(1)}, f32[156,1,6,4]{0,3,2,1:T(4,128)S(1)}, u32[]{:S(2)}, u32[]{:S(2)}) collective-permute-start(f32[156,1,6,4]{0,3,2,1:T(4,128)S(1)} %get-tuple-element.3091), channel_id=1, source_target_pairs={{8,0},{16,8},{24,16},{9,1},{17,9},{25,17},{10,2},{18,10},{26,18},{... | collective-permute-start | bytes 44936 | tf_op jit(solution)/shard_map/ppermute | solution.py:41
  343.9 22.1 %collective-permute-start.18 = (f32[12,1,4,2]{0,3,2,1:T(2,128)S(1)}, f32[12,1,4,2]{0,3,2,1:T(2,128)S(1)}, u32[]{:S(2)}, u32[]{:S(2)}) collective-permute-start(f32[12,1,4,2]{0,3,2,1:T(2,128)S(1)} %bitcast.2227), channel_id=1, source_target_pairs={{8,0},{16,8},{24,16},{9,1},{17,9},{25,17},{10,2},{18,10},{26,18},{... | collective-permute-start | bytes 1160 | tf_op jit(solution)/shard_map/ppermute | solution.py:41
  345.2 20.9 %collective-permute-start.19 = (f32[12,1,4,2]{0,3,2,1:T(2,128)S(1)}, f32[12,1,4,2]{0,3,2,1:T(2,128)S(1)}, u32[]{:S(2)}, u32[]{:S(2)}) collective-permute-start(f32[12,1,4,2]{0,3,2,1:T(2,128)S(1)} %bitcast.2228), channel_id=1, source_target_pairs={{0,8},{8,16},{16,24},{1,9},{9,17},{17,25},{2,10},{10,18},{18,26},{... | collective-permute-start | bytes 1160 | tf_op jit(solution)/shard_map/ppermute | solution.py:40
  360.6 17.0 %collective-permute-start.24 = (f32[12,1,6,4]{0,3,2,1:T(4,128)S(1)}, f32[12,1,6,4]{0,3,2,1:T(4,128)S(1)}, u32[]{:S(2)}, u32[]{:S(2)}) collective-permute-start(f32[12,1,6,4]{0,3,2,1:T(4,128)S(1)} %get-tuple-element.3279), channel_id=1, source_target_pairs={{0,8},{8,16},{16,24},{1,9},{9,17},{17,25},{2,10},{10,18},{18,26},{... | collective-permute-start | bytes 3464 | tf_op jit(solution)/shard_map/ppermute | solution.py:40
  364.6 13.1 %collective-permute-start.25 = (f32[12,1,6,4]{0,3,2,1:T(4,128)S(1)}, f32[12,1,6,4]{0,3,2,1:T(4,128)S(1)}, u32[]{:S(2)}, u32[]{:S(2)}) collective-permute-start(f32[12,1,6,4]{0,3,2,1:T(4,128)S(1)} %get-tuple-element.3280), channel_id=1, source_target_pairs={{8,0},{16,8},{24,16},{9,1},{17,9},{25,17},{10,2},{18,10},{26,18},{... | collective-permute-start | bytes 3464 | tf_op jit(solution)/shard_map/ppermute | solution.py:41
  373.3 19.9 %collective-permute-start.22 = (f32[12,3,6,1]{0,3,2,1:T(1,128)S(1)}, f32[12,3,6,1]{0,3,2,1:T(1,128)S(1)}, u32[]{:S(2)}, u32[]{:S(2)}) collective-permute-start(f32[12,3,6,1]{0,3,2,1:T(1,128)S(1)} %get-tuple-element.3394), channel_id=1, source_target_pairs={{1,0},{3,2},{5,4},{7,6},{9,8},{11,10},{13,12},{15,14},{17,16},{19,... | collective-permute-start | bytes 2600 | tf_op jit(solution)/shard_map/ppermute | solution.py:41
  374.6 18.6 %collective-permute-start.23 = (f32[12,3,6,1]{0,3,2,1:T(1,128)S(1)}, f32[12,3,6,1]{0,3,2,1:T(1,128)S(1)}, u32[]{:S(2)}, u32[]{:S(2)}) collective-permute-start(f32[12,3,6,1]{0,3,2,1:T(1,128)S(1)} %get-tuple-element.3393), channel_id=1, source_target_pairs={{0,1},{2,3},{4,5},{6,7},{8,9},{10,11},{12,13},{14,15},{16,17},{18,... | collective-permute-start | bytes 2600 | tf_op jit(solution)/shard_map/ppermute | solution.py:40
  420.7 19.4 %collective-permute-start.30 = (f32[12,1,4,2]{0,3,2,1:T(2,128)S(1)}, f32[12,1,4,2]{0,3,2,1:T(2,128)S(1)}, u32[]{:S(2)}, u32[]{:S(2)}) collective-permute-start(f32[12,1,4,2]{0,3,2,1:T(2,128)S(1)} %bitcast.2238), channel_id=1, source_target_pairs={{8,0},{16,8},{24,16},{9,1},{17,9},{25,17},{10,2},{18,10},{26,18},{... | collective-permute-start | bytes 1160 | tf_op jit(solution)/shard_map/ppermute | solution.py:41
  422.0 18.1 %collective-permute-start.31 = (f32[12,1,4,2]{0,3,2,1:T(2,128)S(1)}, f32[12,1,4,2]{0,3,2,1:T(2,128)S(1)}, u32[]{:S(2)}, u32[]{:S(2)}) collective-permute-start(f32[12,1,4,2]{0,3,2,1:T(2,128)S(1)} %bitcast.2239), channel_id=1, source_target_pairs={{0,8},{8,16},{16,24},{1,9},{9,17},{17,25},{2,10},{10,18},{18,26},{... | collective-permute-start | bytes 1160 | tf_op jit(solution)/shard_map/ppermute | solution.py:40
  436.7 15.0 %collective-permute-start.36 = (f32[12,1,6,4]{0,3,2,1:T(4,128)S(1)}, f32[12,1,6,4]{0,3,2,1:T(4,128)S(1)}, u32[]{:S(2)}, u32[]{:S(2)}) collective-permute-start(f32[12,1,6,4]{0,3,2,1:T(4,128)S(1)} %get-tuple-element.3277), channel_id=1, source_target_pairs={{0,8},{8,16},{16,24},{1,9},{9,17},{17,25},{2,10},{10,18},{18,26},{... | collective-permute-start | bytes 3464 | tf_op jit(solution)/shard_map/ppermute | solution.py:40
  438.8 12.9 %collective-permute-start.37 = (f32[12,1,6,4]{0,3,2,1:T(4,128)S(1)}, f32[12,1,6,4]{0,3,2,1:T(4,128)S(1)}, u32[]{:S(2)}, u32[]{:S(2)}) collective-permute-start(f32[12,1,6,4]{0,3,2,1:T(4,128)S(1)} %get-tuple-element.3278), channel_id=1, source_target_pairs={{8,0},{16,8},{24,16},{9,1},{17,9},{25,17},{10,2},{18,10},{26,18},{... | collective-permute-start | bytes 3464 | tf_op jit(solution)/shard_map/ppermute | solution.py:41
  447.3 21.0 %collective-permute-start.34 = (f32[12,3,6,1]{0,3,2,1:T(1,128)S(1)}, f32[12,3,6,1]{0,3,2,1:T(1,128)S(1)}, u32[]{:S(2)}, u32[]{:S(2)}) collective-permute-start(f32[12,3,6,1]{0,3,2,1:T(1,128)S(1)} %get-tuple-element.3391), channel_id=1, source_target_pairs={{1,0},{3,2},{5,4},{7,6},{9,8},{11,10},{13,12},{15,14},{17,16},{19,... | collective-permute-start | bytes 2600 | tf_op jit(solution)/shard_map/ppermute | solution.py:41
  448.6 19.7 %collective-permute-start.35 = (f32[12,3,6,1]{0,3,2,1:T(1,128)S(1)}, f32[12,3,6,1]{0,3,2,1:T(1,128)S(1)}, u32[]{:S(2)}, u32[]{:S(2)}) collective-permute-start(f32[12,3,6,1]{0,3,2,1:T(1,128)S(1)} %get-tuple-element.3390), channel_id=1, source_target_pairs={{0,1},{2,3},{4,5},{6,7},{8,9},{10,11},{12,13},{14,15},{16,17},{18,... | collective-permute-start | bytes 2600 | tf_op jit(solution)/shard_map/ppermute | solution.py:40
  499.8 19.3 %collective-permute-start.42 = (f32[12,1,4,2]{0,3,2,1:T(2,128)S(1)}, f32[12,1,4,2]{0,3,2,1:T(2,128)S(1)}, u32[]{:S(2)}, u32[]{:S(2)}) collective-permute-start(f32[12,1,4,2]{0,3,2,1:T(2,128)S(1)} %bitcast.2249), channel_id=1, source_target_pairs={{8,0},{16,8},{24,16},{9,1},{17,9},{25,17},{10,2},{18,10},{26,18},{... | collective-permute-start | bytes 1160 | tf_op jit(solution)/shard_map/ppermute | solution.py:41
  501.1 18.0 %collective-permute-start.43 = (f32[12,1,4,2]{0,3,2,1:T(2,128)S(1)}, f32[12,1,4,2]{0,3,2,1:T(2,128)S(1)}, u32[]{:S(2)}, u32[]{:S(2)}) collective-permute-start(f32[12,1,4,2]{0,3,2,1:T(2,128)S(1)} %bitcast.2250), channel_id=1, source_target_pairs={{0,8},{8,16},{16,24},{1,9},{9,17},{17,25},{2,10},{10,18},{18,26},{... | collective-permute-start | bytes 1160 | tf_op jit(solution)/shard_map/ppermute | solution.py:40
  515.9 14.8 %collective-permute-start.48 = (f32[12,1,6,4]{0,3,2,1:T(4,128)S(1)}, f32[12,1,6,4]{0,3,2,1:T(4,128)S(1)}, u32[]{:S(2)}, u32[]{:S(2)}) collective-permute-start(f32[12,1,6,4]{0,3,2,1:T(4,128)S(1)} %get-tuple-element.3275), channel_id=1, source_target_pairs={{0,8},{8,16},{16,24},{1,9},{9,17},{17,25},{2,10},{10,18},{18,26},{... | collective-permute-start | bytes 3464 | tf_op jit(solution)/shard_map/ppermute | solution.py:40
  517.8 12.9 %collective-permute-start.49 = (f32[12,1,6,4]{0,3,2,1:T(4,128)S(1)}, f32[12,1,6,4]{0,3,2,1:T(4,128)S(1)}, u32[]{:S(2)}, u32[]{:S(2)}) collective-permute-start(f32[12,1,6,4]{0,3,2,1:T(4,128)S(1)} %get-tuple-element.3276), channel_id=1, source_target_pairs={{8,0},{16,8},{24,16},{9,1},{17,9},{25,17},{10,2},{18,10},{26,18},{... | collective-permute-start | bytes 3464 | tf_op jit(solution)/shard_map/ppermute | solution.py:41
  526.3 20.4 %collective-permute-start.46 = (f32[12,3,6,1]{0,3,2,1:T(1,128)S(1)}, f32[12,3,6,1]{0,3,2,1:T(1,128)S(1)}, u32[]{:S(2)}, u32[]{:S(2)}) collective-permute-start(f32[12,3,6,1]{0,3,2,1:T(1,128)S(1)} %get-tuple-element.3388), channel_id=1, source_target_pairs={{1,0},{3,2},{5,4},{7,6},{9,8},{11,10},{13,12},{15,14},{17,16},{19,... | collective-permute-start | bytes 2600 | tf_op jit(solution)/shard_map/ppermute | solution.py:41
  527.6 19.1 %collective-permute-start.47 = (f32[12,3,6,1]{0,3,2,1:T(1,128)S(1)}, f32[12,3,6,1]{0,3,2,1:T(1,128)S(1)}, u32[]{:S(2)}, u32[]{:S(2)}) collective-permute-start(f32[12,3,6,1]{0,3,2,1:T(1,128)S(1)} %get-tuple-element.3387), channel_id=1, source_target_pairs={{0,1},{2,3},{4,5},{6,7},{8,9},{10,11},{12,13},{14,15},{16,17},{18,... | collective-permute-start | bytes 2600 | tf_op jit(solution)/shard_map/ppermute | solution.py:40
  577.4 19.3 %collective-permute-start.54 = (f32[12,1,4,2]{0,3,2,1:T(2,128)S(1)}, f32[12,1,4,2]{0,3,2,1:T(2,128)S(1)}, u32[]{:S(2)}, u32[]{:S(2)}) collective-permute-start(f32[12,1,4,2]{0,3,2,1:T(2,128)S(1)} %bitcast.2260), channel_id=1, source_target_pairs={{8,0},{16,8},{24,16},{9,1},{17,9},{25,17},{10,2},{18,10},{26,18},{... | collective-permute-start | bytes 1160 | tf_op jit(solution)/shard_map/ppermute | solution.py:41
  578.7 18.0 %collective-permute-start.55 = (f32[12,1,4,2]{0,3,2,1:T(2,128)S(1)}, f32[12,1,4,2]{0,3,2,1:T(2,128)S(1)}, u32[]{:S(2)}, u32[]{:S(2)}) collective-permute-start(f32[12,1,4,2]{0,3,2,1:T(2,128)S(1)} %bitcast.2261), channel_id=1, source_target_pairs={{0,8},{8,16},{16,24},{1,9},{9,17},{17,25},{2,10},{10,18},{18,26},{... | collective-permute-start | bytes 1160 | tf_op jit(solution)/shard_map/ppermute | solution.py:40
  593.4 14.8 %collective-permute-start.60 = (f32[12,1,6,4]{0,3,2,1:T(4,128)S(1)}, f32[12,1,6,4]{0,3,2,1:T(4,128)S(1)}, u32[]{:S(2)}, u32[]{:S(2)}) collective-permute-start(f32[12,1,6,4]{0,3,2,1:T(4,128)S(1)} %get-tuple-element.3273), channel_id=1, source_target_pairs={{0,8},{8,16},{16,24},{1,9},{9,17},{17,25},{2,10},{10,18},{18,26},{... | collective-permute-start | bytes 3464 | tf_op jit(solution)/shard_map/ppermute | solution.py:40
  595.3 12.9 %collective-permute-start.61 = (f32[12,1,6,4]{0,3,2,1:T(4,128)S(1)}, f32[12,1,6,4]{0,3,2,1:T(4,128)S(1)}, u32[]{:S(2)}, u32[]{:S(2)}) collective-permute-start(f32[12,1,6,4]{0,3,2,1:T(4,128)S(1)} %get-tuple-element.3274), channel_id=1, source_target_pairs={{8,0},{16,8},{24,16},{9,1},{17,9},{25,17},{10,2},{18,10},{26,18},{... | collective-permute-start | bytes 3464 | tf_op jit(solution)/shard_map/ppermute | solution.py:41
  603.9 20.4 %collective-permute-start.58 = (f32[12,3,6,1]{0,3,2,1:T(1,128)S(1)}, f32[12,3,6,1]{0,3,2,1:T(1,128)S(1)}, u32[]{:S(2)}, u32[]{:S(2)}) collective-permute-start(f32[12,3,6,1]{0,3,2,1:T(1,128)S(1)} %get-tuple-element.3385), channel_id=1, source_target_pairs={{1,0},{3,2},{5,4},{7,6},{9,8},{11,10},{13,12},{15,14},{17,16},{19,... | collective-permute-start | bytes 2600 | tf_op jit(solution)/shard_map/ppermute | solution.py:41
  605.2 19.1 %collective-permute-start.59 = (f32[12,3,6,1]{0,3,2,1:T(1,128)S(1)}, f32[12,3,6,1]{0,3,2,1:T(1,128)S(1)}, u32[]{:S(2)}, u32[]{:S(2)}) collective-permute-start(f32[12,3,6,1]{0,3,2,1:T(1,128)S(1)} %get-tuple-element.3384), channel_id=1, source_target_pairs={{0,1},{2,3},{4,5},{6,7},{8,9},{10,11},{12,13},{14,15},{16,17},{18,... | collective-permute-start | bytes 2600 | tf_op jit(solution)/shard_map/ppermute | solution.py:40
  655.0 19.5 %collective-permute-start.66 = (f32[12,1,4,2]{0,3,2,1:T(2,128)S(1)}, f32[12,1,4,2]{0,3,2,1:T(2,128)S(1)}, u32[]{:S(2)}, u32[]{:S(2)}) collective-permute-start(f32[12,1,4,2]{0,3,2,1:T(2,128)S(1)} %bitcast.2271), channel_id=1, source_target_pairs={{8,0},{16,8},{24,16},{9,1},{17,9},{25,17},{10,2},{18,10},{26,18},{... | collective-permute-start | bytes 1160 | tf_op jit(solution)/shard_map/ppermute | solution.py:41
  656.3 18.2 %collective-permute-start.67 = (f32[12,1,4,2]{0,3,2,1:T(2,128)S(1)}, f32[12,1,4,2]{0,3,2,1:T(2,128)S(1)}, u32[]{:S(2)}, u32[]{:S(2)}) collective-permute-start(f32[12,1,4,2]{0,3,2,1:T(2,128)S(1)} %bitcast.2272), channel_id=1, source_target_pairs={{0,8},{8,16},{16,24},{1,9},{9,17},{17,25},{2,10},{10,18},{18,26},{... | collective-permute-start | bytes 1160 | tf_op jit(solution)/shard_map/ppermute | solution.py:40
  671.2 14.8 %collective-permute-start.72 = (f32[12,1,6,4]{0,3,2,1:T(4,128)S(1)}, f32[12,1,6,4]{0,3,2,1:T(4,128)S(1)}, u32[]{:S(2)}, u32[]{:S(2)}) collective-permute-start(f32[12,1,6,4]{0,3,2,1:T(4,128)S(1)} %get-tuple-element.3271), channel_id=1, source_target_pairs={{0,8},{8,16},{16,24},{1,9},{9,17},{17,25},{2,10},{10,18},{18,26},{... | collective-permute-start | bytes 3464 | tf_op jit(solution)/shard_map/ppermute | solution.py:40
  681.7 20.4 %collective-permute-start.70 = (f32[12,3,6,1]{0,3,2,1:T(1,128)S(1)}, f32[12,3,6,1]{0,3,2,1:T(1,128)S(1)}, u32[]{:S(2)}, u32[]{:S(2)}) collective-permute-start(f32[12,3,6,1]{0,3,2,1:T(1,128)S(1)} %get-tuple-element.3382), channel_id=1, source_target_pairs={{1,0},{3,2},{5,4},{7,6},{9,8},{11,10},{13,12},{15,14},{17,16},{19,... | collective-permute-start | bytes 2600 | tf_op jit(solution)/shard_map/ppermute | solution.py:41
  683.0 19.1 %collective-permute-start.71 = (f32[12,3,6,1]{0,3,2,1:T(1,128)S(1)}, f32[12,3,6,1]{0,3,2,1:T(1,128)S(1)}, u32[]{:S(2)}, u32[]{:S(2)}) collective-permute-start(f32[12,3,6,1]{0,3,2,1:T(1,128)S(1)} %get-tuple-element.3381), channel_id=1, source_target_pairs={{0,1},{2,3},{4,5},{6,7},{8,9},{10,11},{12,13},{14,15},{16,17},{18,... | collective-permute-start | bytes 2600 | tf_op jit(solution)/shard_map/ppermute | solution.py:40
  732.6 19.3 %collective-permute-start.78 = (f32[12,1,4,2]{0,3,2,1:T(2,128)S(1)}, f32[12,1,4,2]{0,3,2,1:T(2,128)S(1)}, u32[]{:S(2)}, u32[]{:S(2)}) collective-permute-start(f32[12,1,4,2]{0,3,2,1:T(2,128)S(1)} %bitcast.2282), channel_id=1, source_target_pairs={{8,0},{16,8},{24,16},{9,1},{17,9},{25,17},{10,2},{18,10},{26,18},{... | collective-permute-start | bytes 1160 | tf_op jit(solution)/shard_map/ppermute | solution.py:41
  733.9 18.0 %collective-permute-start.79 = (f32[12,1,4,2]{0,3,2,1:T(2,128)S(1)}, f32[12,1,4,2]{0,3,2,1:T(2,128)S(1)}, u32[]{:S(2)}, u32[]{:S(2)}) collective-permute-start(f32[12,1,4,2]{0,3,2,1:T(2,128)S(1)} %bitcast.2283), channel_id=1, source_target_pairs={{0,8},{8,16},{16,24},{1,9},{9,17},{17,25},{2,10},{10,18},{18,26},{... | collective-permute-start | bytes 1160 | tf_op jit(solution)/shard_map/ppermute | solution.py:40
  748.6 14.8 %collective-permute-start.84 = (f32[12,1,6,4]{0,3,2,1:T(4,128)S(1)}, f32[12,1,6,4]{0,3,2,1:T(4,128)S(1)}, u32[]{:S(2)}, u32[]{:S(2)}) collective-permute-start(f32[12,1,6,4]{0,3,2,1:T(4,128)S(1)} %get-tuple-element.3269), channel_id=1, source_target_pairs={{0,8},{8,16},{16,24},{1,9},{9,17},{17,25},{2,10},{10,18},{18,26},{... | collective-permute-start | bytes 3464 | tf_op jit(solution)/shard_map/ppermute | solution.py:40
  759.1 20.4 %collective-permute-start.82 = (f32[12,3,6,1]{0,3,2,1:T(1,128)S(1)}, f32[12,3,6,1]{0,3,2,1:T(1,128)S(1)}, u32[]{:S(2)}, u32[]{:S(2)}) collective-permute-start(f32[12,3,6,1]{0,3,2,1:T(1,128)S(1)} %get-tuple-element.3379), channel_id=1, source_target_pairs={{1,0},{3,2},{5,4},{7,6},{9,8},{11,10},{13,12},{15,14},{17,16},{19,... | collective-permute-start | bytes 2600 | tf_op jit(solution)/shard_map/ppermute | solution.py:41
  760.4 19.1 %collective-permute-start.83 = (f32[12,3,6,1]{0,3,2,1:T(1,128)S(1)}, f32[12,3,6,1]{0,3,2,1:T(1,128)S(1)}, u32[]{:S(2)}, u32[]{:S(2)}) collective-permute-start(f32[12,3,6,1]{0,3,2,1:T(1,128)S(1)} %get-tuple-element.3378), channel_id=1, source_target_pairs={{0,1},{2,3},{4,5},{6,7},{8,9},{10,11},{12,13},{14,15},{16,17},{18,... | collective-permute-start | bytes 2600 | tf_op jit(solution)/shard_map/ppermute | solution.py:40
  810.2 19.7 %collective-permute-start.90 = (f32[12,1,4,2]{0,3,2,1:T(2,128)S(1)}, f32[12,1,4,2]{0,3,2,1:T(2,128)S(1)}, u32[]{:S(2)}, u32[]{:S(2)}) collective-permute-start(f32[12,1,4,2]{0,3,2,1:T(2,128)S(1)} %bitcast.2293), channel_id=1, source_target_pairs={{8,0},{16,8},{24,16},{9,1},{17,9},{25,17},{10,2},{18,10},{26,18},{... | collective-permute-start | bytes 1160 | tf_op jit(solution)/shard_map/ppermute | solution.py:41
  811.5 18.4 %collective-permute-start.91 = (f32[12,1,4,2]{0,3,2,1:T(2,128)S(1)}, f32[12,1,4,2]{0,3,2,1:T(2,128)S(1)}, u32[]{:S(2)}, u32[]{:S(2)}) collective-permute-start(f32[12,1,4,2]{0,3,2,1:T(2,128)S(1)} %bitcast.2294), channel_id=1, source_target_pairs={{0,8},{8,16},{16,24},{1,9},{9,17},{17,25},{2,10},{10,18},{18,26},{... | collective-permute-start | bytes 1160 | tf_op jit(solution)/shard_map/ppermute | solution.py:40
  826.6 14.8 %collective-permute-start.96 = (f32[12,1,6,4]{0,3,2,1:T(4,128)S(1)}, f32[12,1,6,4]{0,3,2,1:T(4,128)S(1)}, u32[]{:S(2)}, u32[]{:S(2)}) collective-permute-start(f32[12,1,6,4]{0,3,2,1:T(4,128)S(1)} %get-tuple-element.3267), channel_id=1, source_target_pairs={{0,8},{8,16},{16,24},{1,9},{9,17},{17,25},{2,10},{10,18},{18,26},{... | collective-permute-start | bytes 3464 | tf_op jit(solution)/shard_map/ppermute | solution.py:40
  837.1 20.4 %collective-permute-start.94 = (f32[12,3,6,1]{0,3,2,1:T(1,128)S(1)}, f32[12,3,6,1]{0,3,2,1:T(1,128)S(1)}, u32[]{:S(2)}, u32[]{:S(2)}) collective-permute-start(f32[12,3,6,1]{0,3,2,1:T(1,128)S(1)} %get-tuple-element.3376), channel_id=1, source_target_pairs={{1,0},{3,2},{5,4},{7,6},{9,8},{11,10},{13,12},{15,14},{17,16},{19,... | collective-permute-start | bytes 2600 | tf_op jit(solution)/shard_map/ppermute | solution.py:41
  838.4 19.1 %collective-permute-start.95 = (f32[12,3,6,1]{0,3,2,1:T(1,128)S(1)}, f32[12,3,6,1]{0,3,2,1:T(1,128)S(1)}, u32[]{:S(2)}, u32[]{:S(2)}) collective-permute-start(f32[12,3,6,1]{0,3,2,1:T(1,128)S(1)} %get-tuple-element.3375), channel_id=1, source_target_pairs={{0,1},{2,3},{4,5},{6,7},{8,9},{10,11},{12,13},{14,15},{16,17},{18,... | collective-permute-start | bytes 2600 | tf_op jit(solution)/shard_map/ppermute | solution.py:40
  888.0 19.3 %collective-permute-start.102 = (f32[12,1,4,2]{0,3,2,1:T(2,128)S(1)}, f32[12,1,4,2]{0,3,2,1:T(2,128)S(1)}, u32[]{:S(2)}, u32[]{:S(2)}) collective-permute-start(f32[12,1,4,2]{0,3,2,1:T(2,128)S(1)} %bitcast.2304), channel_id=1, source_target_pairs={{8,0},{16,8},{24,16},{9,1},{17,9},{25,17},{10,2},{18,10},{26,18},{... | collective-permute-start | bytes 1160 | tf_op jit(solution)/shard_map/ppermute | solution.py:41
  889.3 18.0 %collective-permute-start.103 = (f32[12,1,4,2]{0,3,2,1:T(2,128)S(1)}, f32[12,1,4,2]{0,3,2,1:T(2,128)S(1)}, u32[]{:S(2)}, u32[]{:S(2)}) collective-permute-start(f32[12,1,4,2]{0,3,2,1:T(2,128)S(1)} %bitcast.2305), channel_id=1, source_target_pairs={{0,8},{8,16},{16,24},{1,9},{9,17},{17,25},{2,10},{10,18},{18,26},{... | collective-permute-start | bytes 1160 | tf_op jit(solution)/shard_map/ppermute | solution.py:40
  904.1 14.8 %collective-permute-start.108 = (f32[12,1,6,4]{0,3,2,1:T(4,128)S(1)}, f32[12,1,6,4]{0,3,2,1:T(4,128)S(1)}, u32[]{:S(2)}, u32[]{:S(2)}) collective-permute-start(f32[12,1,6,4]{0,3,2,1:T(4,128)S(1)} %get-tuple-element.3265), channel_id=1, source_target_pairs={{0,8},{8,16},{16,24},{1,9},{9,17},{17,25},{2,10},{10,18},{18,26},{... | collective-permute-start | bytes 3464 | tf_op jit(solution)/shard_map/ppermute | solution.py:40
  914.5 20.4 %collective-permute-start.106 = (f32[12,3,6,1]{0,3,2,1:T(1,128)S(1)}, f32[12,3,6,1]{0,3,2,1:T(1,128)S(1)}, u32[]{:S(2)}, u32[]{:S(2)}) collective-permute-start(f32[12,3,6,1]{0,3,2,1:T(1,128)S(1)} %get-tuple-element.3373), channel_id=1, source_target_pairs={{1,0},{3,2},{5,4},{7,6},{9,8},{11,10},{13,12},{15,14},{17,16},{19,... | collective-permute-start | bytes 2600 | tf_op jit(solution)/shard_map/ppermute | solution.py:41
  915.8 19.1 %collective-permute-start.107 = (f32[12,3,6,1]{0,3,2,1:T(1,128)S(1)}, f32[12,3,6,1]{0,3,2,1:T(1,128)S(1)}, u32[]{:S(2)}, u32[]{:S(2)}) collective-permute-start(f32[12,3,6,1]{0,3,2,1:T(1,128)S(1)} %get-tuple-element.3372), channel_id=1, source_target_pairs={{0,1},{2,3},{4,5},{6,7},{8,9},{10,11},{12,13},{14,15},{16,17},{18,... | collective-permute-start | bytes 2600 | tf_op jit(solution)/shard_map/ppermute | solution.py:40
  965.6 19.4 %collective-permute-start.114 = (f32[12,1,4,2]{0,3,2,1:T(2,128)S(1)}, f32[12,1,4,2]{0,3,2,1:T(2,128)S(1)}, u32[]{:S(2)}, u32[]{:S(2)}) collective-permute-start(f32[12,1,4,2]{0,3,2,1:T(2,128)S(1)} %bitcast.2315), channel_id=1, source_target_pairs={{8,0},{16,8},{24,16},{9,1},{17,9},{25,17},{10,2},{18,10},{26,18},{... | collective-permute-start | bytes 1160 | tf_op jit(solution)/shard_map/ppermute | solution.py:41
  966.9 18.1 %collective-permute-start.115 = (f32[12,1,4,2]{0,3,2,1:T(2,128)S(1)}, f32[12,1,4,2]{0,3,2,1:T(2,128)S(1)}, u32[]{:S(2)}, u32[]{:S(2)}) collective-permute-start(f32[12,1,4,2]{0,3,2,1:T(2,128)S(1)} %bitcast.2316), channel_id=1, source_target_pairs={{0,8},{8,16},{16,24},{1,9},{9,17},{17,25},{2,10},{10,18},{18,26},{... | collective-permute-start | bytes 1160 | tf_op jit(solution)/shard_map/ppermute | solution.py:40
  981.8 14.8 %collective-permute-start.120 = (f32[12,1,6,4]{0,3,2,1:T(4,128)S(1)}, f32[12,1,6,4]{0,3,2,1:T(4,128)S(1)}, u32[]{:S(2)}, u32[]{:S(2)}) collective-permute-start(f32[12,1,6,4]{0,3,2,1:T(4,128)S(1)} %get-tuple-element.3263), channel_id=1, source_target_pairs={{0,8},{8,16},{16,24},{1,9},{9,17},{17,25},{2,10},{10,18},{18,26},{... | collective-permute-start | bytes 3464 | tf_op jit(solution)/shard_map/ppermute | solution.py:40
  992.3 20.4 %collective-permute-start.118 = (f32[12,3,6,1]{0,3,2,1:T(1,128)S(1)}, f32[12,3,6,1]{0,3,2,1:T(1,128)S(1)}, u32[]{:S(2)}, u32[]{:S(2)}) collective-permute-start(f32[12,3,6,1]{0,3,2,1:T(1,128)S(1)} %get-tuple-element.3370), channel_id=1, source_target_pairs={{1,0},{3,2},{5,4},{7,6},{9,8},{11,10},{13,12},{15,14},{17,16},{19,... | collective-permute-start | bytes 2600 | tf_op jit(solution)/shard_map/ppermute | solution.py:41
  993.6 19.1 %collective-permute-start.119 = (f32[12,3,6,1]{0,3,2,1:T(1,128)S(1)}, f32[12,3,6,1]{0,3,2,1:T(1,128)S(1)}, u32[]{:S(2)}, u32[]{:S(2)}) collective-permute-start(f32[12,3,6,1]{0,3,2,1:T(1,128)S(1)} %get-tuple-element.3369), channel_id=1, source_target_pairs={{0,1},{2,3},{4,5},{6,7},{8,9},{10,11},{12,13},{14,15},{16,17},{18,... | collective-permute-start | bytes 2600 | tf_op jit(solution)/shard_map/ppermute | solution.py:40
  1043.2 19.3 %collective-permute-start.126 = (f32[12,1,4,2]{0,3,2,1:T(2,128)S(1)}, f32[12,1,4,2]{0,3,2,1:T(2,128)S(1)}, u32[]{:S(2)}, u32[]{:S(2)}) collective-permute-start(f32[12,1,4,2]{0,3,2,1:T(2,128)S(1)} %bitcast.2326), channel_id=1, source_target_pairs={{8,0},{16,8},{24,16},{9,1},{17,9},{25,17},{10,2},{18,10},{26,18},{... | collective-permute-start | bytes 1160 | tf_op jit(solution)/shard_map/ppermute | solution.py:41
  1044.5 18.0 %collective-permute-start.127 = (f32[12,1,4,2]{0,3,2,1:T(2,128)S(1)}, f32[12,1,4,2]{0,3,2,1:T(2,128)S(1)}, u32[]{:S(2)}, u32[]{:S(2)}) collective-permute-start(f32[12,1,4,2]{0,3,2,1:T(2,128)S(1)} %bitcast.2327), channel_id=1, source_target_pairs={{0,8},{8,16},{16,24},{1,9},{9,17},{17,25},{2,10},{10,18},{18,26},{... | collective-permute-start | bytes 1160 | tf_op jit(solution)/shard_map/ppermute | solution.py:40
  1059.3 14.8 %collective-permute-start.132 = (f32[12,1,6,4]{0,3,2,1:T(4,128)S(1)}, f32[12,1,6,4]{0,3,2,1:T(4,128)S(1)}, u32[]{:S(2)}, u32[]{:S(2)}) collective-permute-start(f32[12,1,6,4]{0,3,2,1:T(4,128)S(1)} %get-tuple-element.3261), channel_id=1, source_target_pairs={{0,8},{8,16},{16,24},{1,9},{9,17},{17,25},{2,10},{10,18},{18,26},{... | collective-permute-start | bytes 3464 | tf_op jit(solution)/shard_map/ppermute | solution.py:40
  1069.7 20.4 %collective-permute-start.130 = (f32[12,3,6,1]{0,3,2,1:T(1,128)S(1)}, f32[12,3,6,1]{0,3,2,1:T(1,128)S(1)}, u32[]{:S(2)}, u32[]{:S(2)}) collective-permute-start(f32[12,3,6,1]{0,3,2,1:T(1,128)S(1)} %get-tuple-element.3367), channel_id=1, source_target_pairs={{1,0},{3,2},{5,4},{7,6},{9,8},{11,10},{13,12},{15,14},{17,16},{19,... | collective-permute-start | bytes 2600 | tf_op jit(solution)/shard_map/ppermute | solution.py:41
  1071.0 19.1 %collective-permute-start.131 = (f32[12,3,6,1]{0,3,2,1:T(1,128)S(1)}, f32[12,3,6,1]{0,3,2,1:T(1,128)S(1)}, u32[]{:S(2)}, u32[]{:S(2)}) collective-permute-start(f32[12,3,6,1]{0,3,2,1:T(1,128)S(1)} %get-tuple-element.3366), channel_id=1, source_target_pairs={{0,1},{2,3},{4,5},{6,7},{8,9},{10,11},{12,13},{14,15},{16,17},{18,... | collective-permute-start | bytes 2600 | tf_op jit(solution)/shard_map/ppermute | solution.py:40
  (261 other events, 2380.2 us)
